TPU v7x, 32 devices: a whole 2x2x4 slice. The times are simulated.
32 devices in a mesh: groups: 2 (over y), seq: 4 (over x, core), chan: 4 (over z).
Axes of the slice: x: 2, y: 2, z: 4, core: 2. Of those that a mesh axis runs over, the one named last changes fastest.
Arguments:
- tokens: bfloat16 [4096, 4096], P(('groups', 'seq'), 'chan'), parts along dimension 0, may hold values from -6 to 6
- norm_gain: float32 [4096], replicated, may hold values from 0.5 to 1.5
- proj_weight: bfloat16 [4096, 3, 4096], P('seq', None, 'chan'), may hold values from -0.09375 to 0.09375
- short_filter: float32 [3, 3, 4096], P(None, None, 'chan'), may hold values from -2.5 to 2.5
- long_filter: float32 [4096, 2048], P('chan', 'seq'), may hold values from -4 to 4, as said below
- skip_gain: float32 [4096], P('chan'), may hold values from 0.5 to 1.5
- out_weight: bfloat16 [4096, 4096], P(None, 'chan'), may hold values from -0.09375 to 0.09375
Outputs:
- block_out: bfloat16 [4096, 4096], P(('groups', 'seq'), 'chan'), parts along dimension 0
There are 2 independent parts, one for each index of `groups`. A program takes and returns all parts, laid end to end along the dimension named above; an argument that names none is the same for every part. Nothing has to cross between parts.
Inputs may be any that keep to these rules, and one draw needn't show every extreme that they name: `long_filter`: filter taps of the sequence-long convolution.
All inputs are finite; a program needn't handle non-finite values.
Results may differ from a plain program's by a relative error of at most 0.012.
Values may be sent and summed in bfloat16 or wider, within the bound.
A program may use at most 128 MiB of HBM per device.

v0:
```python
import math

import jax
import jax.numpy as jnp
from jax import lax
from jax.sharding import PartitionSpec as P

SHORT = 3


EPSILON = 1e-06
HIGHEST = lax.Precision.HIGHEST


def from_behind(value, axis, steps):
    count = lax.axis_size(axis)
    initial, last = (max(0, -steps), min(count, count - steps))
    return lax.ppermute(value, axis, [(source, source + steps) for source in range(initial, last)])


def angle_table(row_count, col_count, period, sign):
    row_index = lax.iota(jnp.int32, row_count)[:, None]
    col_index = lax.iota(jnp.int32, col_count)[None, :]
    angles = (row_index * col_index % period).astype(jnp.float32) * (sign * 2.0 * math.pi / period)
    return (jnp.cos(angles), jnp.sin(angles))


def forward_spectrum(signal_rows, first, second):
    channels = signal_rows.shape[0]
    grid_rows = signal_rows.reshape(channels, first, second)
    cos_first, sin_first = angle_table(first, first, first, -1.0)
    part_re = jnp.einsum("cab,ak->ckb", grid_rows, cos_first, precision=HIGHEST)
    part_im = jnp.einsum("cab,ak->ckb", grid_rows, sin_first, precision=HIGHEST)
    twist_cos, twist_sin = angle_table(first, second, first * second, -1.0)
    part_re, part_im = (
        part_re * twist_cos - part_im * twist_sin,
        part_re * twist_sin + part_im * twist_cos,
    )
    cos_second, sin_second = angle_table(second, second, second, -1.0)
    spectrum_real = jnp.einsum("ckb,bm->ckm", part_re, cos_second, precision=HIGHEST) - jnp.einsum(
        "ckb,bm->ckm", part_im, sin_second, precision=HIGHEST
    )
    spec_im = jnp.einsum("ckb,bm->ckm", part_re, sin_second, precision=HIGHEST) + jnp.einsum(
        "ckb,bm->ckm", part_im, cos_second, precision=HIGHEST
    )
    return (spectrum_real, spec_im)


def inverse_spectrum(spectrum_real, spec_im, first, second):
    channels = spectrum_real.shape[0]
    cos_second, sin_second = angle_table(second, second, second, 1.0)
    part_re = jnp.einsum("ckm,bm->ckb", spectrum_real, cos_second, precision=HIGHEST) - jnp.einsum(
        "ckm,bm->ckb", spec_im, sin_second, precision=HIGHEST
    )
    part_im = jnp.einsum("ckm,bm->ckb", spectrum_real, sin_second, precision=HIGHEST) + jnp.einsum(
        "ckm,bm->ckb", spec_im, cos_second, precision=HIGHEST
    )
    twist_cos, twist_sin = angle_table(first, second, first * second, 1.0)
    part_re, part_im = (
        part_re * twist_cos - part_im * twist_sin,
        part_re * twist_sin + part_im * twist_cos,
    )
    cos_first, sin_first = angle_table(first, first, first, 1.0)
    result = jnp.einsum("ckb,ak->cab", part_re, cos_first, precision=HIGHEST) - jnp.einsum(
        "ckb,ak->cab", part_im, sin_first, precision=HIGHEST
    )
    return result.reshape(channels, first * second) / (first * second)


def spectral_conv(signal_rows, filter_rows):
    channels, length = signal_rows.shape
    padded_len = 2 * length
    log_len = padded_len.bit_length() - 1
    first = 1 << log_len // 2
    second = padded_len // first
    zeros_tail = jnp.zeros((channels, length), jnp.float32)
    sig_re, sig_im = forward_spectrum(
        jnp.concatenate([signal_rows, zeros_tail], axis=1), first, second
    )
    tap_re, tap_im = forward_spectrum(
        jnp.concatenate([filter_rows, zeros_tail], axis=1), first, second
    )
    prod_re = sig_re * tap_re - sig_im * tap_im
    prod_im = sig_re * tap_im + sig_im * tap_re
    return inverse_spectrum(prod_re, prod_im, first, second)[:, :length]


def short_filter_output(projected, rim_cells, kernel_coefficients):
    count = kernel_coefficients.shape[0]
    steps_len = projected.shape[2]
    extended = jnp.concatenate([rim_cells, projected], axis=2).astype(jnp.float32)
    total = jnp.zeros(projected.shape, jnp.float32)
    for tap in range(count):
        total = (
            total
            + kernel_coefficients[tap][:, :, None]
            * extended[:, :, count - 1 - tap : count - 1 - tap + steps_len]
        )
    return total.astype(jnp.bfloat16)


def hyena_mixer(keys_rows, values_rows, long_taps, skip_part):
    middle = keys_rows.astype(jnp.float32) * values_rows.astype(jnp.float32)
    return (spectral_conv(middle, long_taps) + skip_part[:, None] * middle).astype(jnp.bfloat16)


def body(tokens, norm_gain, proj_weight, short_filter, long_filter, skip_gain, out_weight):
    seq_count = lax.axis_size("seq")
    local_rows = tokens.shape[0]
    local_chan = proj_weight.shape[2]
    subset = local_chan // seq_count
    length = local_rows * seq_count
    offset = lax.axis_index("seq") * subset
    whole = lax.all_gather(tokens, "chan", axis=1, tiled=True)
    wide = whole.astype(jnp.float32)
    rescaled_signal = (
        wide * lax.rsqrt(jnp.mean(wide * wide, axis=1, keepdims=True) + EPSILON) * norm_gain
    ).astype(jnp.bfloat16)
    projected = lax.dot_general(
        lax.all_gather(proj_weight, "seq", axis=0, tiled=True),
        rescaled_signal,
        (((0,), (1,)), ((), ())),
        preferred_element_type=jnp.float32,
    ).astype(jnp.bfloat16)
    taps_grid = long_filter.reshape(1, seq_count, subset, local_rows)
    long_taps = lax.all_to_all(taps_grid, "seq", split_axis=1, concat_axis=3, tiled=True).reshape(
        subset, length
    )
    skip_part = lax.dynamic_slice_in_dim(skip_gain, offset, subset, 0)
    rim_cells = from_behind(projected[:, :, local_rows - (SHORT - 1) :], "seq", 1)
    featured = short_filter_output(projected, rim_cells, short_filter)
    pair_grid = featured[1:].reshape(2, seq_count, subset, local_rows)
    moved = lax.all_to_all(pair_grid, "seq", split_axis=1, concat_axis=3, tiled=True).reshape(
        2, subset, length
    )
    result = hyena_mixer(moved[0], moved[1], long_taps, skip_part)
    returned = lax.all_to_all(
        result.reshape(1, subset, length), "seq", split_axis=2, concat_axis=0, tiled=True
    )
    returned = returned.reshape(local_chan, local_rows)
    gated = (featured[0].astype(jnp.float32) * returned.astype(jnp.float32)).astype(jnp.bfloat16)
    full_mix = lax.all_gather(gated, "chan", axis=0, tiled=True)
    update = lax.dot_general(
        full_mix, out_weight, (((0,), (0,)), ((), ())), preferred_element_type=jnp.float32
    )
    return (tokens.astype(jnp.float32) + update).astype(jnp.bfloat16)


def solution(mesh):
    placed = (
        P(("groups", "seq"), "chan"),
        P(),
        P("seq", None, "chan"),
        P(None, None, "chan"),
        P("chan", "seq"),
        P("chan"),
        P(None, "chan"),
    )
    return jax.shard_map(
        body, mesh=mesh, in_specs=placed, out_specs=P(("groups", "seq"), "chan"), check_vma=False
    )
```

profile of v0, /device:TPU:0, one launch (start us, length us, event | category | flops | bytes accessed | tf_op | source)
XLA Modules:
  0.0 568.1 jit_solution(13785095065940686060)
XLA Ops:
  12.3 80.1 %all-gather.4.cloned.1.call-done = bf16[512,4096]{1,0:T(8,128)(2,1)} async-done(((bf16[512,1024]{1,0:T(8,128)(2,1)}), bf16[512,4096]{1,0:T(8,128)(2,1)}) %all-gather.4.cloned.1.call-update) | async-done | bytes 4194320 | tf_op jit(solution)/shard_map/all_gather | solution.py:114
  95.5 151.8 %all-gather.6.cloned.1.call-done = bf16[4096,3,1024]{2,0,1:T(8,128)(2,1)} async-done(((bf16[1024,3,1024]{2,0,1:T(8,128)(2,1)}), bf16[4096,3,1024]{2,0,1:T(8,128)(2,1)}) %all-gather.6.cloned.1.call-update) | async-done | bytes 25165840 | tf_op jit(solution)/shard_map/all_gather | solution.py:120
  247.3 18.2 %convert_bitcast_fusion = bf16[3,1024,512]{1,2,0:T(8,128)(2,1)S(1)} fusion(bf16[4096,3,1024]{2,0,1:T(8,128)(2,1)} %all-gather.6.cloned.1.call-done, bf16[512,4096]{1,0:T(8,128)(2,1)} %all-gather.4.cloned.1.call-done, f32[4096]{0:T(1024)S(1)} %copy-done.5, f32[512]{0:T(512)S(1)} %add_rsqrt_fusion), kind=kOutput, calls=%fused_computation.53 | convolution fusion | flops 12894863360 | bytes 32524288 | tf_op jit(solution)/shard_map/dot_general | solution.py:119
  283.4 7.2 %fusion.23 = f32[64,256,64]{1,0,2:T(8,128)} fusion(f32[256,64,64]{0,2,1:T(8,128)S(1)} %bitcast.128), kind=kOutput, calls=%fused_computation.36 | convolution fusion | flops 805363712 | bytes 8388608 | tf_op jit(solution)/shard_map/cab,ak->ckb/dot_general | solution.py:33
  290.6 7.2 %fusion.25 = f32[64,256,64]{1,0,2:T(8,128)} fusion(f32[256,64,64]{0,2,1:T(8,128)S(1)} %bitcast.129), kind=kOutput, calls=%fused_computation.38 | convolution fusion | flops 805363712 | bytes 8388608 | tf_op jit(solution)/shard_map/cab,ak->ckb/dot_general | solution.py:32
  297.7 7.3 %all-to-all-done = bf16[2,4,256,512]{2,3,0,1:T(8,128)(2,1)} async-done(((bf16[2,4,256,512]{2,3,0,1:T(8,128)(2,1)}), bf16[2,4,256,512]{2,3,0,1:T(8,128)(2,1)}, u32[]{:S(2)}, u32[]{:S(2)}) %all-to-all-start) | async-done | bytes 2097184 | tf_op jit(solution)/shard_map/all_to_all | solution.py:133
  309.2 7.1 %fusion.35 = f32[64,256,64]{1,0,2:T(8,128)} fusion(f32[256,64,64]{0,2,1:T(8,128)S(1)} %bitcast.130), kind=kOutput, calls=%fused_computation.48 | convolution fusion | flops 805363712 | bytes 8388608 | tf_op jit(solution)/shard_map/cab,ak->ckb/dot_general | solution.py:33
  316.3 12.5 %subtract_bitcast_fusion = (f32[256,64,64]{0,1,2:T(8,128)S(1)}, f32[256,64,64]{0,1,2:T(8,128)S(1)}, f32[256,64,64]{0,1,2:T(8,128)S(1)}, f32[256,64,64]{0,1,2:T(8,128)S(1)}) fusion(f32[64,256,64]{1,0,2:T(8,128)} %fusion.23, f32[64,256,64]{1,0,2:T(8,128)} %fusion.25, f32[64,64]{0,1:T(8,128)S(1)} %copy.102, f32[64,64]{0,1:T(8,128)S(1)} %copy.99, ...), kind=kOutput, calls=%fused_computation.23 | convolution fusion | flops 817946624 | bytes 33587200 | tf_op jit(solution)/shard_map/cab,ak->ckb/dot_general | solution.py:32
  328.8 6.5 %fusion.15 = f32[256,64,64]{0,2,1:T(8,128)S(1)} fusion(f32[256,64,64]{0,1,2:T(8,128)S(1)} %get-tuple-element.10), kind=kOutput, calls=%fused_computation.28 | convolution fusion | flops 805363712 | bytes 8388608 | tf_op jit(solution)/shard_map/ckb,bm->ckm/dot_general | solution.py:43
  335.3 6.9 %fusion.17 = f32[256,64,64]{0,2,1:T(8,128)S(1)} fusion(f32[256,64,64]{0,1,2:T(8,128)S(1)} %get-tuple-element.10), kind=kOutput, calls=%fused_computation.30 | convolution fusion | flops 805363712 | bytes 8388608 | tf_op jit(solution)/shard_map/ckb,bm->ckm/dot_general | solution.py:40
  342.3 7.3 %fusion.27 = f32[256,64,64]{0,2,1:T(8,128)} fusion(f32[256,64,64]{0,1,2:T(8,128)S(1)} %get-tuple-element.13), kind=kOutput, calls=%fused_computation.40 | convolution fusion | flops 805363712 | bytes 8388608 | tf_op jit(solution)/shard_map/ckb,bm->ckm/dot_general | solution.py:43
  349.6 6.5 %fusion.29 = f32[256,64,64]{0,2,1:T(8,128)S(1)} fusion(f32[256,64,64]{0,1,2:T(8,128)S(1)} %get-tuple-element.13), kind=kOutput, calls=%fused_computation.42 | convolution fusion | flops 805363712 | bytes 8388608 | tf_op jit(solution)/shard_map/ckb,bm->ckm/dot_general | solution.py:40
  356.1 7.3 %fusion.47 = f32[256,64,64]{0,2,1:T(8,128)S(1)} fusion(f32[256,64,64]{0,2,1:T(8,128)S(1)} %fusion.17, f32[256,64,64]{0,1,2:T(8,128)S(1)} %get-tuple-element.9), kind=kOutput, calls=%fused_computation.56 | convolution fusion | flops 806412288 | bytes 12582912 | tf_op jit(solution)/shard_map/ckb,bm->ckm/dot_general | solution.py:40
  363.3 7.4 %fusion.50 = f32[256,64,64]{0,2,1:T(8,128)} fusion(f32[256,64,64]{0,2,1:T(8,128)S(1)} %fusion.15, f32[256,64,64]{0,1,2:T(8,128)S(1)} %get-tuple-element.9), kind=kOutput, calls=%fused_computation.57 | convolution fusion | flops 806412288 | bytes 12582912 | tf_op jit(solution)/shard_map/ckb,bm->ckm/dot_general | solution.py:43
  370.7 7.4 %fusion.41 = f32[256,64,64]{0,2,1:T(8,128)} fusion(f32[256,64,64]{0,2,1:T(8,128)S(1)} %fusion.29, f32[256,64,64]{0,1,2:T(8,128)S(1)} %get-tuple-element.14), kind=kOutput, calls=%fused_computation.54 | convolution fusion | flops 806412288 | bytes 12582912 | tf_op jit(solution)/shard_map/ckb,bm->ckm/dot_general | solution.py:40
  378.1 10.5 %multiply_add_fusion.1 = (f32[256,64,64]{0,2,1:T(8,128)S(1)}, f32[256,64,64]{0,2,1:T(8,128)S(1)}) fusion(f32[256,64,64]{0,2,1:T(8,128)S(1)} %fusion.47, f32[256,64,64]{0,2,1:T(8,128)} %fusion.41, f32[256,64,64]{0,2,1:T(8,128)} %fusion.50, f32[256,64,64]{0,2,1:T(8,128)} %fusion.27, f32[256,64,64]{0,1,2:T(8,128)S(1)} %get-tuple-element.14), kind=kOutput, calls=%fused_computation.20 | convolution fusion | flops 812703744 | bytes 29360128 | tf_op jit(solution)/shard_map/ckb,bm->ckm/dot_general | solution.py:43
  402.2 6.8 %multiply_subtract_fusion = (f32[256,64,64]{0,2,1:T(8,128)S(1)}, f32[256,64,64]{0,2,1:T(8,128)S(1)}) fusion(f32[256,64,64]{0,2,1:T(8,128)S(1)} %convolution_subtract_fusion, f32[64,64]{1,0:T(8,128)S(1)} %get-tuple-element.18, f32[64,64]{1,0:T(8,128)S(1)} %get-tuple-element.19, f32[256,64,64]{0,2,1:T(8,128)S(1)} %fusion.61, ...), kind=kOutput, calls=%fused_computation.19 | convolution fusion | flops 812703744 | bytes 21004288 | tf_op jit(solution)/shard_map/ckm,bm->ckb/dot_general | solution.py:55
  409.0 6.0 %fusion.9 = f32[64,256,64]{1,0,2:T(8,128)S(1)} fusion(f32[256,64,64]{0,2,1:T(8,128)S(1)} %get-tuple-element.8), kind=kOutput, calls=%fused_computation.13 | convolution fusion | flops 805363712 | bytes 8388608 | tf_op jit(solution)/shard_map/ckb,ak->cab/dot_general | solution.py:64
  415.1 6.4 %multiply_bitcast_fusion = f32[256,64,64]{0,1,2:T(8,128)S(1)} fusion(f32[64,256,64]{1,0,2:T(8,128)S(1)} %fusion.9, f32[256,64,64]{0,2,1:T(8,128)S(1)} %get-tuple-element.7), kind=kOutput, calls=%fused_computation.17 | convolution fusion | flops 807460864 | bytes 12582912 | tf_op jit(solution)/shard_map/ckb,ak->cab/dot_general | solution.py:64
  424.3 11.7 %copy.204 = bf16[1,256,2048]{1,0,2:T(2,128)(2,1)S(1)} copy(bf16[1,256,2048]{1,2,0:T(8,128)(2,1)S(1)} %fusion.57) | data formatting | bytes 2097152 | tf_op jit(solution)/shard_map/reshape | solution.py:138
  436.5 10.6 %reduce = bf16[2048,256]{1,0:T(8,128)(2,1)S(1)} reduce(bf16[2048,1,256]{2,1,0:T(2,128)(2,1)S(1)} %bitcast.137, bf16[]{:T(256)} %broadcast.298), dimensions={1}, to_apply=%bitcast.127.reduce_sub_computation | reduce | bytes 2097154
  447.5 17.1 %all_to_all.39 = bf16[4,2,65536]{2,1,0:T(2,128)(2,1)S(1)} all-to-all(bf16[4,2,65536]{2,1,0:T(2,128)(2,1)S(1)} %reshape.133), channel_id=1, replica_groups=mesh['groups'=2,'seq'=4,'chan'=4] {'seq'}, dimensions={0} | all-to-all | bytes 2097152 | tf_op jit(solution)/shard_map/all_to_all | solution.py:137
  470.3 80.9 %all-gather.8.cloned.1.call-done = bf16[4096,512]{0,1:T(8,128)(2,1)} async-done(((bf16[1024,512]{0,1:T(8,128)(2,1)}), bf16[4096,512]{0,1:T(8,128)(2,1)}) %all-gather.8.cloned.1.call-update) | async-done | bytes 4194320 | tf_op jit(solution)/shard_map/all_gather | solution.py:142
  551.2 10.1 %add_convert_fusion = bf16[512,1024]{1,0:T(8,128)(2,1)} fusion(bf16[512,1024]{1,0:T(8,128)(2,1)S(1)} %copy-done.3, bf16[4096,512]{0,1:T(8,128)(2,1)} %all-gather.8.cloned.1.call-done, bf16[4096,1024]{1,0:T(8,128)(2,1)} %param.13), kind=kOutput, calls=%fused_computation.67 | convolution fusion | flops 4296540160 | bytes 14680064 | tf_op jit(solution)/shard_map/dot_general | solution.py:143
  (55 shorter events, 53.7 us)
Async XLA Ops:
  6.5 85.9 %all-gather.4.cloned.1.call-start = ((), (), s32[]{:S(2)}) async-start(), calls=%async_computation.3 | async-start | bytes 5242880 | tf_op jit(solution)/shard_map/all_gather | solution.py:114
  7.3 240.0 %all-gather.6.cloned.1.call-start = ((), (), s32[]{:S(2)}) async-start(), calls=%async_computation.4 | async-start | bytes 31457280 | tf_op jit(solution)/shard_map/all_gather | solution.py:120
  8.0 239.3 %copy-start.5 = (f32[4096]{0:T(1024)S(1)}, f32[4096]{0:T(1024)}, u32[]{:S(2)}) copy-start(f32[4096]{0:T(1024)} %param.8) | copy-start | bytes 49156
  8.0 266.8 %all-to-all-start.1 = ((f32[1,4,256,512]{3,2,0,1:T(8,128)}), f32[1,4,256,512]{3,2,0,1:T(8,128)S(1)}, u32[]{:S(2)}, u32[]{:S(2)}) async-start(f32[1,4,256,512]{3,2,0,1:T(8,128)} %bitcast.143), calls=%async_computation.1 | async-start | bytes 4194304 | tf_op jit(solution)/shard_map/all_to_all | solution.py:126
  95.5 172.2 %copy-start.4 = (f32[3,3,1024]{2,1,0:T(4,128)S(1)}, f32[3,3,1024]{2,1,0:T(4,128)}, u32[]{:S(2)}) copy-start(f32[3,3,1024]{2,1,0:T(4,128)} %param.10) | copy-start | bytes 110596
  265.5 3.0 collective-permute-start
  271.5 1.6 copy-start.1
  274.8 6.2 %copy-start.2 = (f32[1,4,256,512]{3,2,0,1:T(8,128)}, f32[1,4,256,512]{3,2,0,1:T(8,128)S(1)}, u32[]{:S(2)}) copy-start(f32[1,4,256,512]{3,2,0,1:T(8,128)S(1)} %all-to-all-done.1) | copy-start | bytes 6291460
  274.9 30.2 %all-to-all-start = ((bf16[2,4,256,512]{2,3,0,1:T(8,128)(2,1)}), bf16[2,4,256,512]{2,3,0,1:T(8,128)(2,1)}, u32[]{:S(2)}, u32[]{:S(2)}) async-start(bf16[2,4,256,512]{2,3,0,1:T(8,128)(2,1)} %bitcast.136), calls=%async_computation | async-start | bytes 4194304 | tf_op jit(solution)/shard_map/all_to_all | solution.py:133
  279.3 271.9 %all-gather.8.cloned.1.call-start = ((), (), s32[]{:S(2)}) async-start(), calls=%async_computation.5 | async-start | bytes 5242880 | tf_op jit(solution)/shard_map/all_gather | solution.py:142
  307.3 1.9 copy-start
  467.2 84.0 %copy-start.3 = (bf16[512,1024]{1,0:T(8,128)(2,1)S(1)}, bf16[512,1024]{1,0:T(8,128)(2,1)}, u32[]{:S(2)}) copy-start(bf16[512,1024]{1,0:T(8,128)(2,1)} %param.7) | copy-start | bytes 3145732
Sparse Core Ops, SparseCore 0:
  8.9 83.4 all-gather.3
  94.0 153.2 all-gather.5
  470.5 80.7 all-gather.7
where the time goes:
time: 574 us; the launch traced here: 568 us
  waiting for transfers between devices  322 us (56%)
  matrix products  155 us (27%)
  local copies, waits for them, and re-layouts  28.4 us (5%)
  other arithmetic  20.5 us (4%)
  blocking collectives  17.1 us (3%)
  between operations  13.7 us (2%)
  starting transfers between devices  11.4 us (2%)
    all_gather x1, waiting for transfers between devices, body(): lax.all_gather(proj_weight, 'seq', axis=0, tiled=True)  152 us
    all_gather x1, waiting for transfers between devices, body(): full_mix = lax.all_gather(gated, 'chan', axis=0, tiled=True)  80.9 us
    all_gather x1, waiting for transfers between devices, body(): whole = lax.all_gather(tokens, 'chan', axis=1, tiled=True)  80.1 us
    dot_general x2, matrix products, forward_spectrum(): part_re = jnp.einsum('cab,ak->ckb', grid_rows, cos_first, precision=HIGHEST)  19.7 us
    dot_general x1, matrix products, body(): lax.dot_general(lax.all_gather(proj_weight, 'seq', axis=0, tiled=True), r...  18.2 us
    dot_general x2, matrix products, forward_spectrum(): jnp.einsum('ckb,bm->ckm', part_re, sin_second, precision=HIGHEST)  17.9 us
    all_to_all x1, blocking collectives, body(): lax.all_to_all(result.reshape(1, subset, length), 'seq', split_axis=2, co...  17.1 us
    dot_general x2, matrix products, forward_spectrum(): jnp.einsum('ckb,bm->ckm', part_re, cos_second, precision=HIGHEST)  14.6 us
  transfers between devices with their start and end apart: 6, of which 5 were waited for; matrix products, arithmetic and copies ran while one was open for 8% of the time, Pallas kernels for 0%

commit v1 on v0

--- a/solution.py
+++ b/solution.py
@@ -1,8 +1,12 @@
+import functools
 import math
 
 import jax
 import jax.numpy as jnp
+import numpy as np
 from jax import lax
+from jax.experimental import pallas as pl
+from jax.experimental.pallas import tpu as pltpu
 from jax.sharding import PartitionSpec as P
 
 SHORT = 3
@@ -146,6 +150,633 @@
     return (tokens.astype(jnp.float32) + update).astype(jnp.bfloat16)
 
 
+TOKEN_CHUNKS = 8
+WEIGHT_CHUNKS = 8
+ANY = pl.BlockSpec(memory_space=pl.ANY)
+
+
+def remote(src, dst, send_sem, recv_sem, where):
+    return pltpu.make_async_remote_copy(
+        src_ref=src,
+        dst_ref=dst,
+        send_sem=send_sem,
+        recv_sem=recv_sem,
+        device_id=where,
+        device_id_type=pl.DeviceIdType.MESH,
+    )
+
+
+def greet(devices):
+    barrier = pltpu.get_barrier_semaphore()
+    for where, present in devices:
+
+        @pl.when(present)
+        def _():
+            pl.semaphore_signal(
+                barrier, inc=1, device_id=where, device_id_type=pl.DeviceIdType.MESH
+            )
+
+    pl.semaphore_wait(
+        barrier, sum(jnp.asarray(present).astype(jnp.int32) for _, present in devices)
+    )
+
+
+class Line:
+    def __init__(self, view, count, chunks, send_sem, recv_sem, place):
+        self.view, self.count, self.chunks = view, count, chunks
+        self.send_sem, self.recv_sem, self.place = send_sem, recv_sem, place
+        self.me = lax.axis_index("chan")
+
+    def copy(self, way, step, chunk, src=None):
+        step_to = 1 if way == 0 else -1
+        owner = jnp.clip(self.me - step * step_to, 0, self.count - 1)
+        target = jnp.clip(self.me + step_to, 0, self.count - 1)
+        block = self.view(owner, chunk)
+        return remote(
+            block if src is None else src,
+            block,
+            self.send_sem.at[way, step, chunk],
+            self.recv_sem.at[way, step, chunk],
+            self.place(target),
+        )
+
+    def sends(self, way, step):
+        if way == 0:
+            return (self.me - step >= 0) & (self.me + 1 < self.count)
+        return (self.me + step < self.count) & (self.me - 1 >= 0)
+
+    def receives(self, way, step):
+        if way == 0:
+            return self.me - 1 - step >= 0
+        return self.me + 1 + step < self.count
+
+    def arrived(self, way, step, chunk):
+        step_to = 1 if way == 0 else -1
+        owner = jnp.clip(self.me - (step + 1) * step_to, 0, self.count - 1)
+        block = self.view(owner, chunk)
+        remote(
+            block,
+            block,
+            self.send_sem.at[way, step, chunk],
+            self.recv_sem.at[way, step, chunk],
+            self.place(self.me),
+        ).wait_recv()
+        return owner
+
+
+def gather_inputs_kernel(
+    sizes,
+    tokens,
+    weights,
+    taps,
+    all_tokens,
+    all_weights,
+    all_taps,
+    token_room,
+    weight_room,
+    tap_room,
+    local_sem,
+    line_send,
+    line_recv,
+    mate_send,
+    mate_recv,
+    x_send,
+    x_recv,
+    y_send,
+    y_recv,
+    f_send,
+    f_recv,
+):
+    chan_count = sizes
+    y, s, z = (lax.axis_index(name) for name in ("groups", "seq", "chan"))
+    x, core = s // 2, s % 2
+    mate = (y, s + 1 - 2 * core, z)
+    across = lambda to: (y, (1 - x) * 2 + to, z)
+    beside = (1 - y, s, z)
+    rows, width = tokens.shape
+    depth = weights.shape[1]
+    lags = taps.shape[2]
+    half, half_lags = depth // 2, lags // 2
+
+    greet(
+        [
+            (mate, True),
+            (across(0), True),
+            (across(1), True),
+            (beside, True),
+            ((y, s, jnp.minimum(z + 1, chan_count - 1)), z + 1 < chan_count),
+            ((y, s, jnp.maximum(z - 1, 0)), z > 0),
+        ]
+    )
+
+    token_rows = rows // TOKEN_CHUNKS
+    weight_rows = half // WEIGHT_CHUNKS
+
+    def token_view(owner, chunk):
+        return all_tokens.at[
+            pl.ds(core * rows + chunk * token_rows, token_rows), pl.ds(owner * width, width)
+        ]
+
+    line = Line(
+        token_view, chan_count, TOKEN_CHUNKS, line_send, line_recv, lambda to: (y, s, to)
+    )
+
+    def weight_view(owner, part, chunk):
+        return all_weights.at[pl.ds(owner * depth + part * half + chunk * weight_rows, weight_rows)]
+
+    def tap_view(owner, part):
+        return all_taps.at[pl.ds(owner * lags + part * half_lags, half_lags)]
+
+    pending = []
+    for chunk in range(TOKEN_CHUNKS):
+        own = tokens.at[pl.ds(chunk * token_rows, token_rows)]
+        for way in range(2):
+
+            @pl.when(line.sends(way, 0))
+            def _():
+                line.copy(way, 0, chunk, own).start()
+
+        for to in range(2):
+            copy = remote(
+                weights.at[to, pl.ds(y * half + chunk * weight_rows, weight_rows)],
+                weight_view(s, y, chunk),
+                x_send.at[to, chunk],
+                x_recv.at[core, chunk],
+                across(to),
+            )
+            copy.start()
+            pending.append(copy)
+    for to in range(2):
+        copy = remote(
+            taps.at[to, 1 - x, pl.ds(y * half_lags, half_lags)],
+            tap_view(s, y),
+            f_send.at[to],
+            f_recv.at[core],
+            across(to),
+        )
+        copy.start()
+        pending.append(copy)
+    own_view = all_tokens.at[pl.ds(core * rows, rows), pl.ds(z * width, width)]
+    mate_copies = [
+        remote(tokens, own_view, mate_send.at[0], mate_recv.at[0], mate),
+        remote(
+            weights.at[1 - core],
+            all_weights.at[pl.ds(s * depth, depth)],
+            mate_send.at[1],
+            mate_recv.at[1],
+            mate,
+        ),
+        remote(
+            taps.at[1 - core, x],
+            all_taps.at[pl.ds(s * lags, lags)],
+            mate_send.at[2],
+            mate_recv.at[2],
+            mate,
+        ),
+    ]
+    for copy in mate_copies:
+        copy.start()
+    ins = [
+        pltpu.make_async_copy(tokens, token_room, local_sem.at[0]),
+        pltpu.make_async_copy(weights.at[core], weight_room, local_sem.at[1]),
+        pltpu.make_async_copy(taps.at[core, x], tap_room, local_sem.at[2]),
+    ]
+    outs = [
+        pltpu.make_async_copy(token_room, own_view, local_sem.at[3]),
+        pltpu.make_async_copy(
+            weight_room, all_weights.at[pl.ds(s * depth, depth)], local_sem.at[4]
+        ),
+        pltpu.make_async_copy(tap_room, all_taps.at[pl.ds(s * lags, lags)], local_sem.at[5]),
+    ]
+    for copy in ins:
+        copy.start()
+    for first, second in zip(ins, outs):
+        first.wait()
+        second.start()
+
+    def to_mate(way, step, chunk, owner):
+        block = token_view(owner, chunk)
+        index = 3 + (way * (chan_count - 1) + step) * TOKEN_CHUNKS + chunk
+        return remote(block, block, mate_send.at[index], mate_recv.at[index], mate)
+
+    steps = (chan_count - 1) * TOKEN_CHUNKS
+    forwarded = 0
+    for at in range(steps):
+        step, chunk = divmod(at, TOKEN_CHUNKS)
+        for way in range(2):
+
+            @pl.when(line.receives(way, step))
+            def _():
+                owner = line.arrived(way, step, chunk)
+                to_mate(way, step, chunk, owner).start()
+
+            if step + 1 < chan_count - 1:
+
+                @pl.when(line.receives(way, step) & line.sends(way, step + 1))
+                def _():
+                    line.copy(way, step + 1, chunk).start()
+
+        while forwarded * steps < (at + 1) * WEIGHT_CHUNKS and forwarded < WEIGHT_CHUNKS:
+            if (forwarded + 1) * steps > (at + 1) * WEIGHT_CHUNKS:
+                break
+            for origin in range(2):
+                view = weight_view((1 - x) * 2 + origin, y, forwarded)
+                remote(
+                    view, view, x_send.at[origin, forwarded], x_recv.at[origin, forwarded], beside
+                ).wait_recv()
+                copy = remote(
+                    view, view, y_send.at[origin, forwarded], y_recv.at[origin, forwarded], beside
+                )
+                copy.start()
+                pending.append(copy)
+            forwarded += 1
+    for origin in range(2):
+        view = tap_view((1 - x) * 2 + origin, y)
+        remote(view, view, f_send.at[origin], f_recv.at[origin], beside).wait_recv()
+        copy = remote(view, view, f_send.at[2 + origin], f_recv.at[2 + origin], beside)
+        copy.start()
+        pending.append(copy)
+
+    for origin in range(2):
+        owner = (1 - x) * 2 + origin
+        for chunk in range(WEIGHT_CHUNKS):
+            view = weight_view(owner, 1 - y, chunk)
+            remote(
+                view, view, y_send.at[origin, chunk], y_recv.at[origin, chunk], beside
+            ).wait_recv()
+        view = tap_view(owner, 1 - y)
+        remote(view, view, f_send.at[2 + origin], f_recv.at[2 + origin], beside).wait_recv()
+    for copy in outs:
+        copy.wait()
+    for copy in mate_copies:
+        copy.wait_send()
+    other_core = 1 - core
+    mate_s = s + 1 - 2 * core
+    for src, dst, index in (
+        (tokens, all_tokens.at[pl.ds(other_core * rows, rows), pl.ds(z * width, width)], 0),
+        (weights.at[0], all_weights.at[pl.ds(mate_s * depth, depth)], 1),
+        (taps.at[0, 0], all_taps.at[pl.ds(mate_s * lags, lags)], 2),
+    ):
+        remote(src, dst, mate_send.at[index], mate_recv.at[index], mate).wait_recv()
+    for at in range(steps):
+        step, chunk = divmod(at, TOKEN_CHUNKS)
+        for way in range(2):
+
+            @pl.when(line.sends(way, step))
+            def _():
+                line.copy(way, step, chunk).wait_send()
+
+            @pl.when(line.receives(way, step))
+            def _():
+                sign = 1 if way == 0 else -1
+                owner = jnp.clip(z - (step + 1) * sign, 0, chan_count - 1)
+                to_mate(way, step, chunk, owner).wait_send()
+                block = all_tokens.at[
+                    pl.ds(other_core * rows + chunk * token_rows, token_rows),
+                    pl.ds(owner * width, width),
+                ]
+                index = 3 + (way * (chan_count - 1) + step) * TOKEN_CHUNKS + chunk
+                remote(block, block, mate_send.at[index], mate_recv.at[index], mate).wait_recv()
+
+    for copy in pending:
+        copy.wait_send()
+
+
+def gather_inputs(tokens, weights, taps, chan_count):
+    rows, width = tokens.shape
+    _, depth, columns = weights.shape
+    lags, share = taps.shape[2:]
+    mate_count = 3 + 2 * (chan_count - 1) * TOKEN_CHUNKS
+    dma = pltpu.SemaphoreType.DMA
+    return pl.pallas_call(
+        functools.partial(gather_inputs_kernel, chan_count),
+        out_shape=(
+            jax.ShapeDtypeStruct((2 * rows, chan_count * width), tokens.dtype),
+            jax.ShapeDtypeStruct((4 * depth, columns), weights.dtype),
+            jax.ShapeDtypeStruct((4 * lags, share), taps.dtype),
+        ),
+        in_specs=[ANY] * 3,
+        out_specs=[ANY] * 3,
+        scratch_shapes=[
+            pltpu.VMEM((rows, width), tokens.dtype),
+            pltpu.VMEM((depth, columns), weights.dtype),
+            pltpu.VMEM((lags, share), taps.dtype),
+            dma((6,)),
+            dma((2, chan_count - 1, TOKEN_CHUNKS)),
+            dma((2, chan_count - 1, TOKEN_CHUNKS)),
+            dma((mate_count,)),
+            dma((mate_count,)),
+            dma((2, WEIGHT_CHUNKS)),
+            dma((2, WEIGHT_CHUNKS)),
+            dma((2, WEIGHT_CHUNKS)),
+            dma((2, WEIGHT_CHUNKS)),
+            dma((4,)),
+            dma((4,)),
+        ],
+        compiler_params=pltpu.CompilerParams(
+            collective_id=0, has_side_effects=True
+        ),
+        name="gather_inputs",
+    )(tokens, weights, taps)
+
+
+def gather_gated_kernel(
+    chan_count, gated, full, room, local_sem, mate_send, mate_recv, line_send, line_recv
+):
+    y, s, z = (lax.axis_index(name) for name in ("groups", "seq", "chan"))
+    core = s % 2
+    mate = (y, s + 1 - 2 * core, z)
+    _, rows, width = gated.shape
+    half_chunks = TOKEN_CHUNKS // 2
+    chunk_rows = rows // half_chunks
+    greet(
+        [
+            (mate, True),
+            ((y, s, jnp.minimum(z + 1, chan_count - 1)), z + 1 < chan_count),
+            ((y, s, jnp.maximum(z - 1, 0)), z > 0),
+        ]
+    )
+
+    def view(owner, chunk):
+        part, at = divmod(chunk, half_chunks)
+        column = (owner * 2 + (core if part == 0 else 1 - core)) * width
+        return full.at[pl.ds(at * chunk_rows, chunk_rows), pl.ds(column, width)]
+
+    line = Line(view, chan_count, TOKEN_CHUNKS, line_send, line_recv, lambda to: (y, s, to))
+    mine = (z * 2 + core) * width
+    theirs = (z * 2 + 1 - core) * width
+    swap = []
+    for at in range(half_chunks):
+        part = pl.ds(at * chunk_rows, chunk_rows)
+        copy = remote(
+            gated.at[1 - core, part],
+            full.at[part, pl.ds(mine, width)],
+            mate_send.at[at],
+            mate_recv.at[at],
+            mate,
+        )
+        copy.start()
+        swap.append(copy)
+    for chunk in range(half_chunks):
+        own = gated.at[core, pl.ds(chunk * chunk_rows, chunk_rows)]
+        for way in range(2):
+
+            @pl.when(line.sends(way, 0))
+            def _():
+                line.copy(way, 0, chunk, own).start()
+
+    take = pltpu.make_async_copy(gated.at[core], room, local_sem.at[0])
+    take.start()
+    for at in range(half_chunks):
+        part = pl.ds(at * chunk_rows, chunk_rows)
+        block = full.at[part, pl.ds(theirs, width)]
+        remote(block, block, mate_send.at[at], mate_recv.at[at], mate).wait_recv()
+        for way in range(2):
+
+            @pl.when(line.sends(way, 0))
+            def _():
+                line.copy(way, 0, half_chunks + at).start()
+
+    take.wait()
+    put = pltpu.make_async_copy(room, full.at[:, pl.ds(mine, width)], local_sem.at[1])
+    put.start()
+    for step in range(chan_count - 1):
+        for chunk in range(TOKEN_CHUNKS):
+            for way in range(2):
+
+                @pl.when(line.receives(way, step))
+                def _():
+                    line.arrived(way, step, chunk)
+
+                if step + 1 < chan_count - 1:
+
+                    @pl.when(line.receives(way, step) & line.sends(way, step + 1))
+                    def _():
+                        line.copy(way, step + 1, chunk).start()
+
+    put.wait()
+    for copy in swap:
+        copy.wait_send()
+    for step in range(chan_count - 1):
+        for chunk in range(TOKEN_CHUNKS):
+            for way in range(2):
+
+                @pl.when(line.sends(way, step))
+                def _():
+                    line.copy(way, step, chunk).wait_send()
+
+
+def gather_gated(gated, chan_count):
+    _, rows, width = gated.shape
+    dma = pltpu.SemaphoreType.DMA
+    half_chunks = TOKEN_CHUNKS // 2
+    return pl.pallas_call(
+        functools.partial(gather_gated_kernel, chan_count),
+        out_shape=jax.ShapeDtypeStruct((rows, 2 * chan_count * width), gated.dtype),
+        in_specs=[ANY],
+        out_specs=ANY,
+        scratch_shapes=[
+            pltpu.VMEM((rows, width), gated.dtype),
+            dma((2,)),
+            dma((half_chunks,)),
+            dma((half_chunks,)),
+            dma((2, chan_count - 1, TOKEN_CHUNKS)),
+            dma((2, chan_count - 1, TOKEN_CHUNKS)),
+        ],
+        compiler_params=pltpu.CompilerParams(
+            collective_id=1, has_side_effects=True
+        ),
+        name="gather_gated",
+    )(gated)
+
+
+def fourier_tables(length):
+    points = 2 * length
+    first = 1 << ((points.bit_length() - 1) // 2)
+    second = points // first
+    kept = first // 2 + 1
+    padded = -(-2 * kept // 8) * 8
+    low = np.arange(kept)
+    place = second * np.arange(first // 2)[None, :] + np.arange(second)[:, None]
+    angle = (low[None, :, None] * place[:, None, :] % points) * (2 * np.pi / points)
+    outer = np.zeros((second, padded, first // 2))
+    outer[:, :kept] = np.cos(angle)
+    outer[:, kept : 2 * kept] = -np.sin(angle)
+    gain = np.where((low == 0) | (low == first // 2), 1.0, 2.0)[None, None, :] / points
+    back = np.zeros((second, first // 2, padded))
+    back[:, :, :kept] = np.cos(angle).transpose(0, 2, 1) * gain
+    back[:, :, kept : 2 * kept] = -np.sin(angle).transpose(0, 2, 1) * gain
+    inner = (np.arange(second)[:, None] * np.arange(second)[None, :] % second) * (
+        2 * np.pi / second
+    )
+    cos, sin = np.cos(inner), np.sin(inner)
+    ahead = np.block([[cos, sin], [-sin, cos]])
+    behind = np.block([[cos, -sin], [sin, cos]])
+    return first, second, kept, padded, [
+        jnp.asarray(table, jnp.bfloat16) for table in (outer, ahead, behind, back)
+    ]
+
+
+def long_conv_kernel(
+    dims, signal, taps, skip, outer, ahead, behind, back, result, wide, spectra, total
+):
+    first, second, kept, padded = dims
+    length, width = signal.shape
+    reach = first // 2
+    block = 64
+
+    lanes = 128
+    parts = width // lanes
+
+    @pl.loop(0, length // block)
+    def _(at):
+        rows = pl.ds(pl.multiple_of(at * block, block), block)
+        for part in range(parts):
+            cols = pl.ds(part * lanes, lanes)
+            wide[part, rows, :] = signal[rows, cols].astype(jnp.float32)
+            wide[parts + part, rows, :] = taps[rows, cols].astype(jnp.float32)
+
+    for part in range(parts):
+        wide[parts + part, 0:1, :] = (
+            wide[parts + part, 0:1, :] + skip[:, part * lanes : (part + 1) * lanes]
+        )
+
+    @pl.loop(0, second, unroll=2)
+    def _(b):
+        picked = jnp.concatenate(
+            [wide.at[part][pl.ds(b, reach, stride=second), :] for part in range(2 * parts)],
+            axis=1,
+        ).astype(jnp.bfloat16)
+        found = jnp.dot(outer[b], picked, preferred_element_type=jnp.float32)
+        rows = pl.ds(pl.multiple_of(b * padded, 8), padded)
+        for part in range(2 * parts):
+            spectra[part, rows, :] = found[:, part * lanes : (part + 1) * lanes]
+
+    def strided(start):
+        return [
+            spectra.at[part][pl.ds(start, second, stride=padded), :] for part in range(2 * parts)
+        ]
+
+    @pl.loop(0, kept)
+    def _(k):
+        real = jnp.concatenate(strided(k), axis=1)
+        imag = jnp.concatenate(strided(k + kept), axis=1)
+        both = jnp.concatenate([real, imag], axis=0).astype(jnp.bfloat16)
+        freq = jnp.dot(ahead[...], both, preferred_element_type=jnp.float32)
+        sr, si = freq[:second, :width], freq[second:, :width]
+        hr, hi = freq[:second, width:], freq[second:, width:]
+        product = jnp.concatenate([sr * hr - si * hi, sr * hi + si * hr], axis=0)
+        inv = jnp.dot(
+            behind[...], product.astype(jnp.bfloat16), preferred_element_type=jnp.float32
+        )
+        for part in range(parts):
+            cols = slice(part * lanes, (part + 1) * lanes)
+            spectra.at[part][pl.ds(k, second, stride=padded), :] = inv[:second, cols]
+            spectra.at[part][pl.ds(k + kept, second, stride=padded), :] = inv[second:, cols]
+
+    @pl.loop(0, second, unroll=2)
+    def _(b):
+        rows = pl.ds(pl.multiple_of(b * padded, 8), padded)
+        filled = jnp.concatenate([spectra[part, rows, :] for part in range(parts)], axis=1)
+        found = jnp.dot(back[b], filled.astype(jnp.bfloat16), preferred_element_type=jnp.float32)
+        for part in range(parts):
+            total.at[part][pl.ds(b, reach, stride=second), :] = found[
+                :, part * lanes : (part + 1) * lanes
+            ]
+
+    @pl.loop(0, length // block)
+    def _(at):
+        rows = pl.ds(pl.multiple_of(at * block, block), block)
+        for part in range(parts):
+            result[rows, part * lanes : (part + 1) * lanes] = total[part, rows, :].astype(
+                jnp.bfloat16
+            )
+
+
+def long_conv(signal, taps, skip):
+    length, width = signal.shape
+    first, second, kept, padded, tables = fourier_tables(length)
+    return pl.pallas_call(
+        functools.partial(long_conv_kernel, (first, second, kept, padded)),
+        out_shape=jax.ShapeDtypeStruct((length, width), jnp.bfloat16),
+        scratch_shapes=[
+            pltpu.VMEM((2 * width // 128, length, 128), jnp.float32),
+            pltpu.VMEM((2 * width // 128, second * padded, 128), jnp.float32),
+            pltpu.VMEM((width // 128, length, 128), jnp.float32),
+        ],
+        compiler_params=pltpu.CompilerParams(vmem_limit_bytes=56 * 1024 * 1024),
+        name="long_conv",
+    )(signal, taps, skip, *tables)
+
+
+def chip_body(tokens, norm_gain, proj_weight, short_filter, long_filter, skip_gain, out_weight):
+    seq_count, chan_count = lax.axis_size("seq"), lax.axis_size("chan")
+    rows, width = tokens.shape
+    depth, branches, local_chan = proj_weight.shape
+    half = local_chan // 2
+    share = half // 2
+    s = lax.axis_index("seq")
+    x, core = s // 2, s % 2
+    weights = (
+        proj_weight.reshape(depth, branches, 2, half)
+        .transpose(2, 0, 1, 3)
+        .reshape(2, depth, branches * half)
+    )
+    taps = (
+        long_filter.astype(jnp.bfloat16).reshape(2, 2, share, rows).transpose(0, 1, 3, 2)
+    )
+    whole, all_weights, all_taps = gather_inputs(tokens, weights, taps, chan_count)
+    wide = whole.astype(jnp.float32)
+    normed = (
+        wide * lax.rsqrt(jnp.mean(wide * wide, axis=1, keepdims=True) + EPSILON) * norm_gain
+    ).astype(jnp.bfloat16)
+    projected = jnp.dot(normed, all_weights, preferred_element_type=jnp.float32).astype(
+        jnp.bfloat16
+    )
+    rim = from_behind(projected[-(SHORT - 1) :], "seq", 2)
+    short = lax.dynamic_slice_in_dim(short_filter, core * half, half, 2).reshape(
+        SHORT, branches * half
+    )
+    extended = jnp.concatenate([rim, projected], axis=0).astype(jnp.float32)
+    featured = jnp.zeros(projected.shape, jnp.float32)
+    for tap in range(SHORT):
+        start = SHORT - 1 - tap
+        featured = featured + short[tap] * extended[start : start + projected.shape[0]]
+    featured = featured.astype(jnp.bfloat16)
+    middle = (
+        featured[:, half : 2 * half].astype(jnp.float32)
+        * featured[:, 2 * half :].astype(jnp.float32)
+    ).astype(jnp.bfloat16)
+    swap = [(at, (at + 2) % seq_count) for at in range(seq_count)]
+    near = x == 0
+    left, right = middle[:, :share], middle[:, share:]
+    kept = jnp.where(near, left, right)
+    other = lax.ppermute(jnp.where(near, right, left), "seq", swap)
+    signal = jnp.concatenate(
+        [jnp.where(near, kept, other), jnp.where(near, other, kept)], axis=0
+    )
+    skip = lax.dynamic_slice_in_dim(skip_gain, core * half + x * share, share, 0)
+    longer = long_conv(signal, all_taps, skip[None, :])
+    early, late = longer[: 2 * rows], longer[2 * rows :]
+    kept = jnp.where(near, early, late)
+    other = lax.ppermute(jnp.where(near, late, early), "seq", swap)
+    longer = jnp.concatenate(
+        [jnp.where(near, kept, other), jnp.where(near, other, kept)], axis=1
+    )
+    gated = (featured[:, :half].astype(jnp.float32) * longer.astype(jnp.float32)).astype(
+        jnp.bfloat16
+    )
+    full_mix = gather_gated(gated.reshape(2, rows, half), chan_count)
+    update = jnp.dot(full_mix, out_weight, preferred_element_type=jnp.float32)
+    return (tokens.astype(jnp.float32) + update).astype(jnp.bfloat16)
+
+
+def select_body(mesh):
+    if mesh.shape["seq"] == 4 and mesh.shape["groups"] == 2:
+        return chip_body
+    return body
+
+
 def solution(mesh):
     placed = (
         P(("groups", "seq"), "chan"),
@@ -157,5 +788,5 @@
         P(None, "chan"),
     )
     return jax.shard_map(
-        body, mesh=mesh, in_specs=placed, out_specs=P(("groups", "seq"), "chan"), check_vma=False
-    )
+        select_body(mesh), mesh=mesh, in_specs=placed, out_specs=P(("groups", "seq"), "chan"), check_vma=False
+    )

time: 574 us -> 295 us (0.51)
  waiting for transfers between devices: 322 us -> 20.5 us
  Pallas kernels: 0 us -> 196 us
  matrix products: 155 us -> 26.2 us
  blocking collectives: 17.1 us -> 0 us
  between operations: 13.7 us -> 0.19 us
    all_gather x3 -> x0, waiting for transfers between devices: 313 us -> none  [the longest x1 152 us: body(): lax.all_gather(proj_weight, 'seq', axis=0, tiled=True)]
    pallas_call x0 -> x3, Pallas kernels: none -> 196 us  [the longest x1 93.3 us: gather_inputs(): pl.pallas_call(functools.partial(gather_inputs_kernel, chan_count), out_s...]
    dot_general x20 -> x2, matrix products: 155 us -> 26.2 us  [the longest x1 15.9 us: chip_body(): jnp.dot(normed, all_weights, preferred_element_type=jnp.float32)]
    ppermute x0 -> x2, waiting for transfers between devices: none -> 19.5 us  [the longest x1 9.93 us: chip_body(): other = lax.ppermute(jnp.where(near, late, early), 'seq', swap)]
    all_to_all x1 -> x0, blocking collectives: 17.1 us -> none  [body(): lax.all_to_all(result.reshape(1, subset, length), 'seq', split_axis=2, co...]
    unnamed x1 -> x0, other arithmetic: 10.6 us -> none
    all_to_all x2 -> x0, starting transfers between devices: 8.69 us -> none  [the longest x1 4.44 us: body(): lax.all_to_all(pair_grid, 'seq', split_axis=1, concat_axis=3, tiled=True)]
    all_to_all x2 -> x0, waiting for transfers between devices: 7.31 us -> none  [the longest x1 7.31 us: body(): lax.all_to_all(pair_grid, 'seq', split_axis=1, concat_axis=3, tiled=True)]
  transfers between devices with their start and end apart: 6 -> 3, of which waited for: 5 -> 3; matrix products, arithmetic and copies ran while one was open for 8% -> 0% of each run, Pallas kernels for 0% -> 0%
where the time goes in v1:
time: 295 us; the launch traced here: 294 us
  Pallas kernels  196 us (66%)
  local copies, waits for them, and re-layouts  28.4 us (10%)
  matrix products  26.2 us (9%)
  waiting for transfers between devices  20.5 us (7%)
  other arithmetic  15.7 us (5%)
  starting transfers between devices  6.73 us (2%)
    pallas_call x1, Pallas kernels, gather_inputs(): pl.pallas_call(functools.partial(gather_inputs_kernel, chan_count), out_s...  93.3 us
    pallas_call x1, Pallas kernels, gather_gated(): pl.pallas_call(functools.partial(gather_gated_kernel, chan_count), out_sh...  72.8 us
    pallas_call x1, Pallas kernels, long_conv(): pl.pallas_call(functools.partial(long_conv_kernel, (first, second, kept,...  30.1 us
    dot_general x1, matrix products, chip_body(): jnp.dot(normed, all_weights, preferred_element_type=jnp.float32)  15.9 us
    dot_general x1, matrix products, chip_body(): update = jnp.dot(full_mix, out_weight, preferred_element_type=jnp.float32)  10.3 us
    unnamed x11, local copies, waits for them, and re-layouts  10.2 us
    ppermute x1, waiting for transfers between devices, chip_body(): other = lax.ppermute(jnp.where(near, late, early), 'seq', swap)  9.93 us
    ppermute x1, waiting for transfers between devices, chip_body(): other = lax.ppermute(jnp.where(near, right, left), 'seq', swap)  9.52 us
  transfers between devices with their start and end apart: 3, of which 3 were waited for; matrix products, arithmetic and copies ran while one was open for 0% of the time, Pallas kernels for 0%

profile of v1, /device:TPU:0, one launch (start us, length us, event | category | flops | bytes accessed | tf_op | source)
XLA Modules:
  0.0 293.9 jit_solution(2758296021710859323)
XLA Ops:
  0.0 8.7 %copy.15 = bf16[1024,3,1024]{0,2,1:T(8,128)(2,1)} copy(bf16[1024,3,1024]{2,0,1:T(8,128)(2,1)} %param.13) | data formatting | bytes 12582912 | tf_op args[2]
  8.7 6.8 %copy.16 = bf16[2,1024,3,512]{1,3,2,0:T(8,128)(2,1)} copy(bf16[2,1024,3,512]{1,3,0,2:T(8,128)(2,1)} %bitcast.12) | data formatting | bytes 12582912 | tf_op jit(solution)/shard_map/transpose | solution.py:722
  15.5 8.8 %copy.18.weights = bf16[2,1024,1536]{2,1,0:T(8,128)(2,1)} copy(bf16[2,1024,1536]{1,2,0:T(8,128)(2,1)} %bitcast.11) | data formatting | bytes 12582912 | tf_op jit(solution)/shard_map/reshape | solution.py:723
  24.4 1.3 copy.17
  25.7 93.3 %gather_inputs.1 = (bf16[1024,4096]{1,0:T(8,128)(2,1)}, bf16[4096,1536]{1,0:T(8,128)(2,1)}, bf16[2048,256]{1,0:T(8,128)(2,1)}) custom-call(bf16[512,1024]{1,0:T(8,128)(2,1)} %tokens.1, bf16[2,1024,1536]{2,1,0:T(8,128)(2,1)} %copy.18.weights, bf16[2,2,512,256]{3,2,1,0:T(8,128)(2,1)} %bitcast.15), custom_call_target="tpu_custom_call" | custom-call | tf_op jit(solution)/shard_map/gather_inputs/pallas_call | solution.py:451
  119.1 5.2 %fusion = f32[1024]{0:T(1024)S(1)} fusion(bf16[1024,4096]{1,0:T(8,128)(2,1)} %get-tuple-element.8), kind=kLoop, calls=%fused_computation.2 | loop fusion | flops 12581888 | bytes 8392704 | tf_op jit(solution)/shard_map/reduce_sum | solution.py:731
  124.8 15.9 %fusion.10 = bf16[1024,1536]{1,0:T(8,128)(2,1)S(1)} fusion(bf16[4096,1536]{1,0:T(8,128)(2,1)} %get-tuple-element.9, bf16[1024,4096]{1,0:T(8,128)(2,1)S(1)} %copy-done.1, f32[4096]{0:T(1024)S(1)} %copy-done.4, f32[1024]{0:T(1024)S(1)} %add_rsqrt_fusion), kind=kOutput, calls=%fused_computation.14 | convolution fusion | flops 12903251968 | bytes 24137728 | tf_op jit(solution)/shard_map/dot_general | solution.py:733
  140.8 2.6 collective-permute-start
  143.5 1.0 collective-permute-done
  145.5 2.0 fusion.8
  147.8 1.0 copy-done
  149.6 2.3 collective-permute-start.1
  151.9 1.3 dynamic_slice.7
  153.2 9.5 %collective-permute-done.1 = bf16[1024,256]{1,0:T(8,128)(2,1)} collective-permute-done((bf16[1024,256]{1,0:T(8,128)(2,1)}, bf16[1024,256]{1,0:T(8,128)(2,1)}, u32[]{:S(2)}, u32[]{:S(2)}) %collective-permute-start.1) | collective-permute-done | bytes 524320 | tf_op jit(solution)/shard_map/ppermute | solution.py:754
  162.7 1.4 broadcast_select_fusion.5
  164.2 1.0 pad_maximum_fusion.signal
  165.2 30.1 %long_conv.1 = bf16[2048,256]{1,0:T(8,128)(2,1)} custom-call(bf16[2048,256]{1,0:T(8,128)(2,1)} %pad_maximum_fusion.signal, bf16[2048,256]{1,0:T(8,128)(2,1)} %get-tuple-element.10.taps, f32[1,256]{1,0:T(1,128)} %bitcast.16, bf16[64,72,32]{2,1,0:T(8,128)(2,1)} %constant.51.clone.outer, bf16[128,128]{1,0:T(8,128)(2,1)} %constant.52.clone.ahead, ...), custom_call_target="tpu_custom_call" | custom-call | tf_op jit(solution)/shard_map/long_conv/pallas_call | solution.py:699
  195.3 1.3 broadcast_select_fusion.2
  196.5 1.8 collective-permute-start.2
  198.4 9.9 %collective-permute-done.2 = bf16[1024,256]{1,0:T(8,128)(2,1)S(1)} collective-permute-done((bf16[1024,256]{1,0:T(8,128)(2,1)S(1)}, bf16[1024,256]{1,0:T(8,128)(2,1)S(1)}, u32[]{:S(2)}, u32[]{:S(2)}) %collective-permute-start.2) | collective-permute-done | bytes 524320 | tf_op jit(solution)/shard_map/ppermute | solution.py:762
  208.3 1.3 broadcast_select_fusion.1
  209.6 1.3 multiply_convert_fusion
  210.8 72.8 %gather_gated.1 = bf16[512,4096]{1,0:T(8,128)(2,1)} custom-call(bf16[2,512,512]{2,1,0:T(8,128)(2,1)} %bitcast.13), custom_call_target="tpu_custom_call" | custom-call | tf_op jit(solution)/shard_map/gather_gated/pallas_call | solution.py:573
  283.6 10.3 %add_convert_fusion = bf16[512,1024]{1,0:T(8,128)(2,1)} fusion(bf16[512,1024]{1,0:T(8,128)(2,1)} %tokens.1, bf16[512,4096]{1,0:T(8,128)(2,1)} %gather_gated.1, bf16[4096,1024]{1,0:T(8,128)(2,1)} %param.17), kind=kOutput, calls=%fused_computation.16 | convolution fusion | flops 4296540160 | bytes 14680064 | tf_op jit(solution)/shard_map/dot_general | solution.py:770
  (19 shorter events, 2.8 us)
Async XLA Ops:
  15.5 8.8 %copy-start.2 = (f32[1024,512]{1,0:T(8,128)S(1)}, f32[1024,512]{1,0:T(8,128)}, u32[]{:S(2)}) copy-start(f32[1024,512]{1,0:T(8,128)} %param.15) | copy-start | bytes 6291460
  25.7 98.6 %copy-start.4 = (f32[4096]{0:T(1024)S(1)}, f32[4096]{0:T(1024)}, u32[]{:S(2)}) copy-start(f32[4096]{0:T(1024)} %param.12) | copy-start | bytes 49156
  119.1 5.8 %copy-start.1 = (bf16[1024,4096]{1,0:T(8,128)(2,1)S(1)}, bf16[1024,4096]{1,0:T(8,128)(2,1)}, u32[]{:S(2)}) copy-start(bf16[1024,4096]{1,0:T(8,128)(2,1)} %get-tuple-element.8) | copy-start | bytes 25165828
  124.8 18.6 %copy-start.3 = (f32[3,3,1024]{2,1,0:T(4,128)S(1)}, f32[3,3,1024]{2,1,0:T(4,128)}, u32[]{:S(2)}) copy-start(f32[3,3,1024]{2,1,0:T(4,128)} %param.14) | copy-start | bytes 110596
  140.8 3.8 %collective-permute-start = (bf16[2,1536]{1,0:T(2,128)(2,1)S(1)}, bf16[2,1536]{1,0:T(2,128)(2,1)S(1)}, u32[]{:S(2)}, u32[]{:S(2)}) collective-permute-start(bf16[2,1536]{1,0:T(2,128)(2,1)S(1)} %slice.59), channel_id=1, source_target_pairs={{0,8},{4,12},{1,9},{5,13},{2,10},{6,14},{3,11},{7,15},{16,24},{20,... | collective-permute-start | bytes 18440 | tf_op jit(solution)/shard_map/ppermute | solution.py:22
  147.8 1.0 copy-start
  149.6 13.1 %collective-permute-start.1 = (bf16[1024,256]{1,0:T(8,128)(2,1)}, bf16[1024,256]{1,0:T(8,128)(2,1)}, u32[]{:S(2)}, u32[]{:S(2)}) collective-permute-start(bf16[1024,256]{1,0:T(8,128)(2,1)} %broadcast_select_fusion.6), channel_id=1, source_target_pairs={{0,8},{4,12},{8,0},{12,4},{1,9},{5,13},{9,1},{13,5},{2,10},{6,14},... | collective-permute-start | bytes 1572872 | tf_op jit(solution)/shard_map/ppermute | solution.py:754
  196.5 11.7 %collective-permute-start.2 = (bf16[1024,256]{1,0:T(8,128)(2,1)S(1)}, bf16[1024,256]{1,0:T(8,128)(2,1)S(1)}, u32[]{:S(2)}, u32[]{:S(2)}) collective-permute-start(bf16[1024,256]{1,0:T(8,128)(2,1)S(1)} %broadcast_select_fusion.2), channel_id=1, source_target_pairs={{0,8},{4,12},{8,0},{12,4},{1,9},{5,13},{9,1},{13,5},{2,10},{6,14},... | collective-permute-start | bytes 1572872 | tf_op jit(solution)/shard_map/ppermute | solution.py:762

commit v2 on v1

--- a/solution.py
+++ b/solution.py
@@ -151,7 +151,7 @@
 
 
 TOKEN_CHUNKS = 8
-WEIGHT_CHUNKS = 8
+WEIGHT_CHUNKS = 16
 ANY = pl.BlockSpec(memory_space=pl.ANY)
 
 
@@ -254,7 +254,7 @@
     across = lambda to: (y, (1 - x) * 2 + to, z)
     beside = (1 - y, s, z)
     rows, width = tokens.shape
-    depth = weights.shape[1]
+    branches, depth, columns = weights.shape[0], weights.shape[1], weights.shape[2] // 2
     lags = taps.shape[2]
     half, half_lags = depth // 2, lags // 2
 
@@ -296,16 +296,24 @@
             def _():
                 line.copy(way, 0, chunk, own).start()
 
+    for chunk in range(WEIGHT_CHUNKS):
         for to in range(2):
-            copy = remote(
-                weights.at[to, pl.ds(y * half + chunk * weight_rows, weight_rows)],
-                weight_view(s, y, chunk),
-                x_send.at[to, chunk],
-                x_recv.at[core, chunk],
-                across(to),
+            view = weight_view(s, y, chunk)
+            for b in range(branches):
+                remote(
+                    weights.at[
+                        b,
+                        pl.ds(y * half + chunk * weight_rows, weight_rows),
+                        pl.ds(to * columns, columns),
+                    ],
+                    view.at[:, pl.ds(b * columns, columns)],
+                    x_send.at[to, chunk],
+                    x_recv.at[core, chunk],
+                    across(to),
+                ).start()
+            pending.append(
+                remote(view, view, x_send.at[to, chunk], x_recv.at[core, chunk], across(to))
             )
-            copy.start()
-            pending.append(copy)
     for to in range(2):
         copy = remote(
             taps.at[to, 1 - x, pl.ds(y * half_lags, half_lags)],
@@ -320,7 +328,7 @@
     mate_copies = [
         remote(tokens, own_view, mate_send.at[0], mate_recv.at[0], mate),
         remote(
-            weights.at[1 - core],
+            all_weights.at[pl.ds(s * depth, depth)],
             all_weights.at[pl.ds(s * depth, depth)],
             mate_send.at[1],
             mate_recv.at[1],
@@ -334,19 +342,37 @@
             mate,
         ),
     ]
-    for copy in mate_copies:
+    for copy in (mate_copies[0], mate_copies[2]):
         copy.start()
+    for b in range(branches):
+        remote(
+            weights.at[b, :, pl.ds((1 - core) * columns, columns)],
+            all_weights.at[pl.ds(s * depth, depth), pl.ds(b * columns, columns)],
+            mate_send.at[1],
+            mate_recv.at[1],
+            mate,
+        ).start()
     ins = [
         pltpu.make_async_copy(tokens, token_room, local_sem.at[0]),
-        pltpu.make_async_copy(weights.at[core], weight_room, local_sem.at[1]),
-        pltpu.make_async_copy(taps.at[core, x], tap_room, local_sem.at[2]),
+        pltpu.make_async_copy(taps.at[core, x], tap_room, local_sem.at[1]),
+    ] + [
+        pltpu.make_async_copy(
+            weights.at[b, :, pl.ds(core * columns, columns)],
+            weight_room.at[:, pl.ds(b * columns, columns)],
+            local_sem.at[2 + b],
+        )
+        for b in range(branches)
     ]
     outs = [
-        pltpu.make_async_copy(token_room, own_view, local_sem.at[3]),
+        pltpu.make_async_copy(token_room, own_view, local_sem.at[5]),
+        pltpu.make_async_copy(tap_room, all_taps.at[pl.ds(s * lags, lags)], local_sem.at[6]),
+    ] + [
         pltpu.make_async_copy(
-            weight_room, all_weights.at[pl.ds(s * depth, depth)], local_sem.at[4]
-        ),
-        pltpu.make_async_copy(tap_room, all_taps.at[pl.ds(s * lags, lags)], local_sem.at[5]),
+            weight_room.at[:, pl.ds(b * columns, columns)],
+            all_weights.at[pl.ds(s * depth, depth), pl.ds(b * columns, columns)],
+            local_sem.at[7 + b],
+        )
+        for b in range(branches)
     ]
     for copy in ins:
         copy.start()
@@ -414,7 +440,11 @@
     mate_s = s + 1 - 2 * core
     for src, dst, index in (
         (tokens, all_tokens.at[pl.ds(other_core * rows, rows), pl.ds(z * width, width)], 0),
-        (weights.at[0], all_weights.at[pl.ds(mate_s * depth, depth)], 1),
+        (
+            all_weights.at[pl.ds(mate_s * depth, depth)],
+            all_weights.at[pl.ds(mate_s * depth, depth)],
+            1,
+        ),
         (taps.at[0, 0], all_taps.at[pl.ds(mate_s * lags, lags)], 2),
     ):
         remote(src, dst, mate_send.at[index], mate_recv.at[index], mate).wait_recv()
@@ -444,7 +474,8 @@
 
 def gather_inputs(tokens, weights, taps, chan_count):
     rows, width = tokens.shape
-    _, depth, columns = weights.shape
+    branches, depth, both = weights.shape
+    columns = branches * both // 2
     lags, share = taps.shape[2:]
     mate_count = 3 + 2 * (chan_count - 1) * TOKEN_CHUNKS
     dma = pltpu.SemaphoreType.DMA
@@ -461,7 +492,7 @@
             pltpu.VMEM((rows, width), tokens.dtype),
             pltpu.VMEM((depth, columns), weights.dtype),
             pltpu.VMEM((lags, share), taps.dtype),
-            dma((6,)),
+            dma((10,)),
             dma((2, chan_count - 1, TOKEN_CHUNKS)),
             dma((2, chan_count - 1, TOKEN_CHUNKS)),
             dma((mate_count,)),
@@ -641,7 +672,7 @@
             wide[parts + part, 0:1, :] + skip[:, part * lanes : (part + 1) * lanes]
         )
 
-    @pl.loop(0, second, unroll=2)
+    @pl.loop(0, second, unroll=4)
     def _(b):
         picked = jnp.concatenate(
             [wide.at[part][pl.ds(b, reach, stride=second), :] for part in range(2 * parts)],
@@ -657,7 +688,7 @@
             spectra.at[part][pl.ds(start, second, stride=padded), :] for part in range(2 * parts)
         ]
 
-    @pl.loop(0, kept)
+    @pl.loop(0, kept, unroll=3)
     def _(k):
         real = jnp.concatenate(strided(k), axis=1)
         imag = jnp.concatenate(strided(k + kept), axis=1)
@@ -674,7 +705,7 @@
             spectra.at[part][pl.ds(k, second, stride=padded), :] = inv[:second, cols]
             spectra.at[part][pl.ds(k + kept, second, stride=padded), :] = inv[second:, cols]
 
-    @pl.loop(0, second, unroll=2)
+    @pl.loop(0, second, unroll=4)
     def _(b):
         rows = pl.ds(pl.multiple_of(b * padded, 8), padded)
         filled = jnp.concatenate([spectra[part, rows, :] for part in range(parts)], axis=1)
@@ -705,6 +736,9 @@
             pltpu.VMEM((width // 128, length, 128), jnp.float32),
         ],
         compiler_params=pltpu.CompilerParams(vmem_limit_bytes=56 * 1024 * 1024),
+        cost_estimate=pl.CostEstimate(
+            flops=2 * 64 * length * width * 40, bytes_accessed=6 * length * width, transcendentals=0
+        ),
         name="long_conv",
     )(signal, taps, skip, *tables)
 
@@ -717,11 +751,7 @@
     share = half // 2
     s = lax.axis_index("seq")
     x, core = s // 2, s % 2
-    weights = (
-        proj_weight.reshape(depth, branches, 2, half)
-        .transpose(2, 0, 1, 3)
-        .reshape(2, depth, branches * half)
-    )
+    weights = proj_weight.transpose(1, 0, 2)
     taps = (
         long_filter.astype(jnp.bfloat16).reshape(2, 2, share, rows).transpose(0, 1, 3, 2)
     )
@@ -749,20 +779,23 @@
     ).astype(jnp.bfloat16)
     swap = [(at, (at + 2) % seq_count) for at in range(seq_count)]
     near = x == 0
-    left, right = middle[:, :share], middle[:, share:]
-    kept = jnp.where(near, left, right)
-    other = lax.ppermute(jnp.where(near, right, left), "seq", swap)
-    signal = jnp.concatenate(
-        [jnp.where(near, kept, other), jnp.where(near, other, kept)], axis=0
-    )
     skip = lax.dynamic_slice_in_dim(skip_gain, core * half + x * share, share, 0)
-    longer = long_conv(signal, all_taps, skip[None, :])
-    early, late = longer[: 2 * rows], longer[2 * rows :]
-    kept = jnp.where(near, early, late)
-    other = lax.ppermute(jnp.where(near, late, early), "seq", swap)
-    longer = jnp.concatenate(
-        [jnp.where(near, kept, other), jnp.where(near, other, kept)], axis=1
-    )
+    lanes = 128
+    found = []
+    for at in range(share // lanes):
+        cols = slice(at * lanes, (at + 1) * lanes)
+        left, right = middle[:, cols], middle[:, share:][:, cols]
+        kept = jnp.where(near, left, right)
+        other = lax.ppermute(jnp.where(near, right, left), "seq", swap)
+        signal = jnp.concatenate(
+            [jnp.where(near, kept, other), jnp.where(near, other, kept)], axis=0
+        )
+        longer = long_conv(signal, all_taps[:, cols], skip[None, cols])
+        early, late = longer[: 2 * rows], longer[2 * rows :]
+        kept = jnp.where(near, early, late)
+        other = lax.ppermute(jnp.where(near, late, early), "seq", swap)
+        found.append((jnp.where(near, kept, other), jnp.where(near, other, kept)))
+    longer = jnp.concatenate([part[0] for part in found] + [part[1] for part in found], axis=1)
     gated = (featured[:, :half].astype(jnp.float32) * longer.astype(jnp.float32)).astype(
         jnp.bfloat16
     )

time: 295 us -> 264 us (0.89)
  local copies, waits for them, and re-layouts: 28.4 us -> 5.36 us
  waiting for transfers between devices: 20.5 us -> 8.54 us
  starting transfers between devices: 6.73 us -> 9.69 us
    reshape x1 -> x0, local copies, waits for them, and re-layouts: 8.76 us -> none  [chip_body(): weights = proj_weight.reshape(depth, branches, 2, half).transpose(2, 0, 1...]
    unnamed x11 -> x14, local copies, waits for them, and re-layouts: 10.2 us -> 1.5 us
    transpose x1 -> x0, local copies, waits for them, and re-layouts: 6.84 us -> none  [chip_body(): weights = proj_weight.reshape(depth, branches, 2, half).transpose(2, 0, 1...]
    ppermute x1 -> x2, waiting for transfers between devices: 9.52 us -> 2.94 us  [chip_body(): other = lax.ppermute(jnp.where(near, right, left), 'seq', swap)]
    ppermute x1 -> x2, waiting for transfers between devices: 9.93 us -> 4.57 us  [chip_body(): other = lax.ppermute(jnp.where(near, late, early), 'seq', swap)]
    pallas_call x1, Pallas kernels: 93.3 us -> 89.9 us  [gather_inputs(): pl.pallas_call(functools.partial(gather_inputs_kernel, chan_count), out_s...]
    pallas_call x1 -> x2, Pallas kernels: 30.1 us -> 33.4 us  [long_conv(): pl.pallas_call(functools.partial(long_conv_kernel, (first, second, kept,...]
  transfers between devices with their start and end apart: 3 -> 5, of which waited for: 3 -> 3; matrix products, arithmetic and copies ran while one was open for 0% -> 2% of each run, Pallas kernels for 0% -> 13%
where the time goes in v2:
time: 264 us
  Pallas kernels  195 us (74%)
  matrix products  26.2 us (10%)
  other arithmetic  18.6 us (7%)
  starting transfers between devices  9.69 us (4%)
  waiting for transfers between devices  8.54 us (3%)
  local copies, waits for them, and re-layouts  5.36 us (2%)
    pallas_call x1, Pallas kernels, gather_inputs(): pl.pallas_call(functools.partial(gather_inputs_kernel, chan_count), out_s...  89.9 us
    pallas_call x1, Pallas kernels, gather_gated(): pl.pallas_call(functools.partial(gather_gated_kernel, chan_count), out_sh...  71.7 us
    pallas_call x2, Pallas kernels, long_conv(): pl.pallas_call(functools.partial(long_conv_kernel, (first, second, kept,...  33.4 us
    dot_general x1, matrix products, chip_body(): jnp.dot(normed, all_weights, preferred_element_type=jnp.float32)  15.9 us
    dot_general x1, matrix products, chip_body(): update = jnp.dot(full_mix, out_weight, preferred_element_type=jnp.float32)  10.3 us
  transfers between devices with their start and end apart: 5, of which 3 were waited for; matrix products, arithmetic and copies ran while one was open for 2% of the time, Pallas kernels for 13%

profile of v2, /device:TPU:0, one launch (start us, length us, event | category | flops | bytes accessed | tf_op | source)
XLA Modules:
  0.0 263.6 jit_solution(16801270220319080360)
XLA Ops:
  0.0 1.7 convert_element_type.43
  1.7 1.3 copy.16
  3.0 89.9 %gather_inputs.1 = (bf16[1024,4096]{1,0:T(8,128)(2,1)}, bf16[4096,1536]{1,0:T(8,128)(2,1)}, bf16[2048,256]{1,0:T(8,128)(2,1)}) custom-call(bf16[512,1024]{1,0:T(8,128)(2,1)} %tokens.1, bf16[3,1024,1024]{2,1,0:T(8,128)(2,1)} %bitcast.11, bf16[2,2,512,256]{3,2,1,0:T(8,128)(2,1)} %bitcast.14), custom_call_target="tpu_custom_call" | custom-call | tf_op jit(solution)/shard_map/gather_inputs/pallas_call | solution.py:482
  93.0 5.2 %fusion = f32[1024]{0:T(1024)S(1)} fusion(bf16[1024,4096]{1,0:T(8,128)(2,1)} %get-tuple-element.8), kind=kLoop, calls=%fused_computation.2 | loop fusion | flops 12581888 | bytes 8392704 | tf_op jit(solution)/shard_map/reduce_sum | solution.py:761
  98.7 15.9 %fusion.10 = bf16[1024,1536]{1,0:T(8,128)(2,1)S(1)} fusion(bf16[4096,1536]{1,0:T(8,128)(2,1)} %get-tuple-element.9, bf16[1024,4096]{1,0:T(8,128)(2,1)S(1)} %copy-done.2, f32[4096]{0:T(1024)S(1)} %copy-done.6, f32[1024]{0:T(1024)S(1)} %add_rsqrt_fusion), kind=kOutput, calls=%fused_computation.14 | convolution fusion | flops 12903251968 | bytes 24137728 | tf_op jit(solution)/shard_map/dot_general | solution.py:763
  114.7 3.4 %collective-permute-start = (bf16[2,1536]{1,0:T(2,128)(2,1)S(1)}, bf16[2,1536]{1,0:T(2,128)(2,1)S(1)}, u32[]{:S(2)}, u32[]{:S(2)}) collective-permute-start(bf16[2,1536]{1,0:T(2,128)(2,1)S(1)} %slice.95), channel_id=1, source_target_pairs={{0,8},{4,12},{1,9},{5,13},{2,10},{6,14},{3,11},{7,15},{16,24},{20,... | collective-permute-start | bytes 18440 | tf_op jit(solution)/shard_map/ppermute | solution.py:22
  118.2 1.0 collective-permute-done
  120.2 2.0 fusion.8
  122.5 1.0 copy-done
  124.3 2.3 collective-permute-start.1
  126.5 1.1 fusion.13
  129.0 2.9 %collective-permute-done.1 = bf16[1024,128]{1,0:T(8,128)(2,1)S(1)} collective-permute-done((bf16[1024,128]{1,0:T(8,128)(2,1)}, bf16[1024,128]{1,0:T(8,128)(2,1)S(1)}, u32[]{:S(2)}, u32[]{:S(2)}) %collective-permute-start.1) | collective-permute-done | bytes 262176 | tf_op jit(solution)/shard_map/ppermute | solution.py:789
  132.0 1.3 broadcast_select_fusion.13
  133.3 1.8 collective-permute-start.3
  135.9 16.7 %long_conv.2 = bf16[2048,128]{1,0:T(8,128)(2,1)} custom-call(bf16[2048,128]{1,0:T(8,128)(2,1)} %pad_maximum_fusion.signal, bf16[2048,128]{1,0:T(8,128)(2,1)} %get-tuple-element.15.taps, f32[1,128]{1,0:T(1,128)} %get-tuple-element.25.skip, bf16[64,72,32]{2,1,0:T(8,128)(2,1)} %constant.51.clone.outer, bf16[128,128]{1,0:T(8,128)(2,1)} %constant.52.clone.ahead, ...), custom_call_target="tpu_custom_call" | custom-call | flops 1342177280 | bytes 1572864 | tf_op jit(solution)/shard_map/long_conv/pallas_call | solution.py:730
  152.6 1.1 broadcast_select_fusion.10
  155.0 16.7 %long_conv.3 = bf16[2048,128]{1,0:T(8,128)(2,1)} custom-call(bf16[2048,128]{1,0:T(8,128)(2,1)} %pad_maximum_fusion.1.signal, bf16[2048,128]{1,0:T(8,128)(2,1)} %get-tuple-element.16.taps, f32[1,128]{1,0:T(1,128)} %get-tuple-element.26.skip, bf16[64,72,32]{2,1,0:T(8,128)(2,1)} %constant.51.clone.outer, bf16[128,128]{1,0:T(8,128)(2,1)} %constant.52.clone.ahead, ...), custom_call_target="tpu_custom_call" | custom-call | flops 1342177280 | bytes 1572864 | tf_op jit(solution)/shard_map/long_conv/pallas_call | solution.py:730
  171.7 1.1 broadcast_select_fusion.3
  172.7 1.8 collective-permute-start.4
  174.6 4.6 %collective-permute-done.4 = bf16[1024,128]{1,0:T(8,128)(2,1)S(1)} collective-permute-done((bf16[1024,128]{1,0:T(8,128)(2,1)S(1)}, bf16[1024,128]{1,0:T(8,128)(2,1)S(1)}, u32[]{:S(2)}, u32[]{:S(2)}) %collective-permute-start.4) | collective-permute-done | bytes 262176 | tf_op jit(solution)/shard_map/ppermute | solution.py:796
  179.2 1.1 broadcast_select_fusion.2
  180.3 1.3 multiply_convert_fusion
  181.6 71.7 %gather_gated.1 = bf16[512,4096]{1,0:T(8,128)(2,1)} custom-call(bf16[2,512,512]{2,1,0:T(8,128)(2,1)} %bitcast.12), custom_call_target="tpu_custom_call" | custom-call | tf_op jit(solution)/shard_map/gather_gated/pallas_call | solution.py:604
  253.3 10.3 %add_convert_fusion = bf16[512,1024]{1,0:T(8,128)(2,1)} fusion(bf16[512,1024]{1,0:T(8,128)(2,1)} %tokens.1, bf16[512,4096]{1,0:T(8,128)(2,1)} %gather_gated.1, bf16[4096,1024]{1,0:T(8,128)(2,1)} %param.21), kind=kOutput, calls=%fused_computation.16 | convolution fusion | flops 4296540160 | bytes 14680064 | tf_op jit(solution)/shard_map/dot_general | solution.py:803
  (31 shorter events, 6.2 us)
Async XLA Ops:
  3.0 95.2 %copy-start.6 = (f32[4096]{0:T(1024)S(1)}, f32[4096]{0:T(1024)}, u32[]{:S(2)}) copy-start(f32[4096]{0:T(1024)} %param.16) | copy-start | bytes 49156
  93.0 5.8 %copy-start.2 = (bf16[1024,4096]{1,0:T(8,128)(2,1)S(1)}, bf16[1024,4096]{1,0:T(8,128)(2,1)}, u32[]{:S(2)}) copy-start(bf16[1024,4096]{1,0:T(8,128)(2,1)} %get-tuple-element.8) | copy-start | bytes 25165828
  98.7 19.4 %copy-start.5 = (f32[3,3,1024]{2,1,0:T(4,128)S(1)}, f32[3,3,1024]{2,1,0:T(4,128)}, u32[]{:S(2)}) copy-start(f32[3,3,1024]{2,1,0:T(4,128)} %param.18) | copy-start | bytes 110596
  114.7 4.6 %collective-permute-start = (bf16[2,1536]{1,0:T(2,128)(2,1)S(1)}, bf16[2,1536]{1,0:T(2,128)(2,1)S(1)}, u32[]{:S(2)}, u32[]{:S(2)}) collective-permute-start(bf16[2,1536]{1,0:T(2,128)(2,1)S(1)} %slice.95), channel_id=1, source_target_pairs={{0,8},{4,12},{1,9},{5,13},{2,10},{6,14},{3,11},{7,15},{16,24},{20,... | collective-permute-start | bytes 18440 | tf_op jit(solution)/shard_map/ppermute | solution.py:22
  120.2 6.3 %copy-start.4 = (bf16[2048,256]{1,0:T(8,128)(2,1)S(1)}, bf16[2048,256]{1,0:T(8,128)(2,1)}, u32[]{:S(2)}) copy-start(bf16[2048,256]{1,0:T(8,128)(2,1)} %get-tuple-element.10) | copy-start | bytes 3145732
  122.5 1.0 copy-start
  124.3 7.7 %collective-permute-start.1 = (bf16[1024,128]{1,0:T(8,128)(2,1)}, bf16[1024,128]{1,0:T(8,128)(2,1)S(1)}, u32[]{:S(2)}, u32[]{:S(2)}) collective-permute-start(bf16[1024,128]{1,0:T(8,128)(2,1)} %broadcast_select_fusion.14), channel_id=1, source_target_pairs={{0,8},{4,12},{8,0},{12,4},{1,9},{5,13},{9,1},{13,5},{2,10},{6,14},... | collective-permute-start | bytes 786440 | tf_op jit(solution)/shard_map/ppermute | solution.py:789
  127.6 26.5 %copy-start.1 = (bf16[1024,512]{1,0:T(8,128)(2,1)S(1)}, bf16[1024,512]{1,0:T(8,128)(2,1)}, u32[]{:S(2)}) copy-start(bf16[1024,512]{1,0:T(8,128)(2,1)} %copy-done) | copy-start | bytes 3145732
  133.3 20.8 %collective-permute-start.3 = (bf16[1024,128]{1,0:T(8,128)(2,1)S(1)}, bf16[1024,128]{1,0:T(8,128)(2,1)S(1)}, u32[]{:S(2)}, u32[]{:S(2)}) collective-permute-start(bf16[1024,128]{1,0:T(8,128)(2,1)S(1)} %get-tuple-element.17), channel_id=1, source_target_pairs={{0,8},{4,12},{8,0},{12,4},{1,9},{5,13},{9,1},{13,5},{2,10},{6,14},... | collective-permute-start | bytes 786440 | tf_op jit(solution)/shard_map/ppermute | solution.py:789
  152.6 21.9 %copy-start.3 = (bf16[2048,128]{1,0:T(8,128)(2,1)S(1)}, bf16[2048,128]{1,0:T(8,128)(2,1)}, u32[]{:S(2)}) copy-start(bf16[2048,128]{1,0:T(8,128)(2,1)} %long_conv.2) | copy-start | bytes 1572868
  153.8 20.8 %collective-permute-start.2 = (bf16[1024,128]{1,0:T(8,128)(2,1)S(1)}, bf16[1024,128]{1,0:T(8,128)(2,1)S(1)}, u32[]{:S(2)}, u32[]{:S(2)}) collective-permute-start(bf16[1024,128]{1,0:T(8,128)(2,1)S(1)} %broadcast_select_fusion.10), channel_id=1, source_target_pairs={{0,8},{4,12},{8,0},{12,4},{1,9},{5,13},{9,1},{13,5},{2,10},{6,14},... | collective-permute-start | bytes 786440 | tf_op jit(solution)/shard_map/ppermute | solution.py:796
  172.7 6.4 %collective-permute-start.4 = (bf16[1024,128]{1,0:T(8,128)(2,1)S(1)}, bf16[1024,128]{1,0:T(8,128)(2,1)S(1)}, u32[]{:S(2)}, u32[]{:S(2)}) collective-permute-start(bf16[1024,128]{1,0:T(8,128)(2,1)S(1)} %broadcast_select_fusion.3), channel_id=1, source_target_pairs={{0,8},{4,12},{8,0},{12,4},{1,9},{5,13},{9,1},{13,5},{2,10},{6,14},... | collective-permute-start | bytes 786440 | tf_op jit(solution)/shard_map/ppermute | solution.py:796

commit v3 on v2

--- a/solution.py
+++ b/solution.py
@@ -152,6 +152,7 @@
 
 TOKEN_CHUNKS = 8
 WEIGHT_CHUNKS = 16
+GATED_CHUNKS = 4
 ANY = pl.BlockSpec(memory_space=pl.ANY)
 
 
@@ -511,116 +512,6 @@
     )(tokens, weights, taps)
 
 
-def gather_gated_kernel(
-    chan_count, gated, full, room, local_sem, mate_send, mate_recv, line_send, line_recv
-):
-    y, s, z = (lax.axis_index(name) for name in ("groups", "seq", "chan"))
-    core = s % 2
-    mate = (y, s + 1 - 2 * core, z)
-    _, rows, width = gated.shape
-    half_chunks = TOKEN_CHUNKS // 2
-    chunk_rows = rows // half_chunks
-    greet(
-        [
-            (mate, True),
-            ((y, s, jnp.minimum(z + 1, chan_count - 1)), z + 1 < chan_count),
-            ((y, s, jnp.maximum(z - 1, 0)), z > 0),
-        ]
-    )
-
-    def view(owner, chunk):
-        part, at = divmod(chunk, half_chunks)
-        column = (owner * 2 + (core if part == 0 else 1 - core)) * width
-        return full.at[pl.ds(at * chunk_rows, chunk_rows), pl.ds(column, width)]
-
-    line = Line(view, chan_count, TOKEN_CHUNKS, line_send, line_recv, lambda to: (y, s, to))
-    mine = (z * 2 + core) * width
-    theirs = (z * 2 + 1 - core) * width
-    swap = []
-    for at in range(half_chunks):
-        part = pl.ds(at * chunk_rows, chunk_rows)
-        copy = remote(
-            gated.at[1 - core, part],
-            full.at[part, pl.ds(mine, width)],
-            mate_send.at[at],
-            mate_recv.at[at],
-            mate,
-        )
-        copy.start()
-        swap.append(copy)
-    for chunk in range(half_chunks):
-        own = gated.at[core, pl.ds(chunk * chunk_rows, chunk_rows)]
-        for way in range(2):
-
-            @pl.when(line.sends(way, 0))
-            def _():
-                line.copy(way, 0, chunk, own).start()
-
-    take = pltpu.make_async_copy(gated.at[core], room, local_sem.at[0])
-    take.start()
-    for at in range(half_chunks):
-        part = pl.ds(at * chunk_rows, chunk_rows)
-        block = full.at[part, pl.ds(theirs, width)]
-        remote(block, block, mate_send.at[at], mate_recv.at[at], mate).wait_recv()
-        for way in range(2):
-
-            @pl.when(line.sends(way, 0))
-            def _():
-                line.copy(way, 0, half_chunks + at).start()
-
-    take.wait()
-    put = pltpu.make_async_copy(room, full.at[:, pl.ds(mine, width)], local_sem.at[1])
-    put.start()
-    for step in range(chan_count - 1):
-        for chunk in range(TOKEN_CHUNKS):
-            for way in range(2):
-
-                @pl.when(line.receives(way, step))
-                def _():
-                    line.arrived(way, step, chunk)
-
-                if step + 1 < chan_count - 1:
-
-                    @pl.when(line.receives(way, step) & line.sends(way, step + 1))
-                    def _():
-                        line.copy(way, step + 1, chunk).start()
-
-    put.wait()
-    for copy in swap:
-        copy.wait_send()
-    for step in range(chan_count - 1):
-        for chunk in range(TOKEN_CHUNKS):
-            for way in range(2):
-
-                @pl.when(line.sends(way, step))
-                def _():
-                    line.copy(way, step, chunk).wait_send()
-
-
-def gather_gated(gated, chan_count):
-    _, rows, width = gated.shape
-    dma = pltpu.SemaphoreType.DMA
-    half_chunks = TOKEN_CHUNKS // 2
-    return pl.pallas_call(
-        functools.partial(gather_gated_kernel, chan_count),
-        out_shape=jax.ShapeDtypeStruct((rows, 2 * chan_count * width), gated.dtype),
-        in_specs=[ANY],
-        out_specs=ANY,
-        scratch_shapes=[
-            pltpu.VMEM((rows, width), gated.dtype),
-            dma((2,)),
-            dma((half_chunks,)),
-            dma((half_chunks,)),
-            dma((2, chan_count - 1, TOKEN_CHUNKS)),
-            dma((2, chan_count - 1, TOKEN_CHUNKS)),
-        ],
-        compiler_params=pltpu.CompilerParams(
-            collective_id=1, has_side_effects=True
-        ),
-        name="gather_gated",
-    )(gated)
-
-
 def fourier_tables(length):
     points = 2 * length
     first = 1 << ((points.bit_length() - 1) // 2)
@@ -648,80 +539,92 @@
     ]
 
 
-def long_conv_kernel(
+def conv_phases(
     dims, signal, taps, skip, outer, ahead, behind, back, result, wide, spectra, total
 ):
     first, second, kept, padded = dims
     length, width = signal.shape
     reach = first // 2
     block = 64
-
     lanes = 128
     parts = width // lanes
 
-    @pl.loop(0, length // block)
-    def _(at):
-        rows = pl.ds(pl.multiple_of(at * block, block), block)
+    lanes = 128
+    parts = width // lanes
+
+    def ahead_outer():
+        @pl.loop(0, length // block)
+        def _(at):
+            rows = pl.ds(pl.multiple_of(at * block, block), block)
+            for part in range(parts):
+                cols = pl.ds(part * lanes, lanes)
+                wide[part, rows, :] = signal[rows, cols].astype(jnp.float32)
+                wide[parts + part, rows, :] = taps[rows, cols].astype(jnp.float32)
+
         for part in range(parts):
-            cols = pl.ds(part * lanes, lanes)
-            wide[part, rows, :] = signal[rows, cols].astype(jnp.float32)
-            wide[parts + part, rows, :] = taps[rows, cols].astype(jnp.float32)
-
-    for part in range(parts):
-        wide[parts + part, 0:1, :] = (
-            wide[parts + part, 0:1, :] + skip[:, part * lanes : (part + 1) * lanes]
-        )
-
-    @pl.loop(0, second, unroll=4)
-    def _(b):
-        picked = jnp.concatenate(
-            [wide.at[part][pl.ds(b, reach, stride=second), :] for part in range(2 * parts)],
-            axis=1,
-        ).astype(jnp.bfloat16)
-        found = jnp.dot(outer[b], picked, preferred_element_type=jnp.float32)
-        rows = pl.ds(pl.multiple_of(b * padded, 8), padded)
-        for part in range(2 * parts):
-            spectra[part, rows, :] = found[:, part * lanes : (part + 1) * lanes]
-
-    def strided(start):
-        return [
-            spectra.at[part][pl.ds(start, second, stride=padded), :] for part in range(2 * parts)
-        ]
-
-    @pl.loop(0, kept, unroll=3)
-    def _(k):
-        real = jnp.concatenate(strided(k), axis=1)
-        imag = jnp.concatenate(strided(k + kept), axis=1)
-        both = jnp.concatenate([real, imag], axis=0).astype(jnp.bfloat16)
-        freq = jnp.dot(ahead[...], both, preferred_element_type=jnp.float32)
-        sr, si = freq[:second, :width], freq[second:, :width]
-        hr, hi = freq[:second, width:], freq[second:, width:]
-        product = jnp.concatenate([sr * hr - si * hi, sr * hi + si * hr], axis=0)
-        inv = jnp.dot(
-            behind[...], product.astype(jnp.bfloat16), preferred_element_type=jnp.float32
-        )
-        for part in range(parts):
-            cols = slice(part * lanes, (part + 1) * lanes)
-            spectra.at[part][pl.ds(k, second, stride=padded), :] = inv[:second, cols]
-            spectra.at[part][pl.ds(k + kept, second, stride=padded), :] = inv[second:, cols]
-
-    @pl.loop(0, second, unroll=4)
-    def _(b):
-        rows = pl.ds(pl.multiple_of(b * padded, 8), padded)
-        filled = jnp.concatenate([spectra[part, rows, :] for part in range(parts)], axis=1)
-        found = jnp.dot(back[b], filled.astype(jnp.bfloat16), preferred_element_type=jnp.float32)
-        for part in range(parts):
-            total.at[part][pl.ds(b, reach, stride=second), :] = found[
-                :, part * lanes : (part + 1) * lanes
+            wide[parts + part, 0:1, :] = (
+                wide[parts + part, 0:1, :] + skip[:, part * lanes : (part + 1) * lanes]
+            )
+
+        @pl.loop(0, second, unroll=4)
+        def _(b):
+            picked = jnp.concatenate(
+                [wide.at[part][pl.ds(b, reach, stride=second), :] for part in range(2 * parts)],
+                axis=1,
+            ).astype(jnp.bfloat16)
+            found = jnp.dot(outer[b], picked, preferred_element_type=jnp.float32)
+            rows = pl.ds(pl.multiple_of(b * padded, 8), padded)
+            for part in range(2 * parts):
+                spectra[part, rows, :] = found[:, part * lanes : (part + 1) * lanes]
+
+    def inner():
+        def strided(start):
+            return [
+                spectra.at[part][pl.ds(start, second, stride=padded), :] for part in range(2 * parts)
             ]
 
-    @pl.loop(0, length // block)
-    def _(at):
-        rows = pl.ds(pl.multiple_of(at * block, block), block)
-        for part in range(parts):
-            result[rows, part * lanes : (part + 1) * lanes] = total[part, rows, :].astype(
-                jnp.bfloat16
+        @pl.loop(0, kept, unroll=3)
+        def _(k):
+            real = jnp.concatenate(strided(k), axis=1)
+            imag = jnp.concatenate(strided(k + kept), axis=1)
+            both = jnp.concatenate([real, imag], axis=0).astype(jnp.bfloat16)
+            freq = jnp.dot(ahead[...], both, preferred_element_type=jnp.float32)
+            sr, si = freq[:second, :width], freq[second:, :width]
+            hr, hi = freq[:second, width:], freq[second:, width:]
+            product = jnp.concatenate([sr * hr - si * hi, sr * hi + si * hr], axis=0)
+            inv = jnp.dot(
+                behind[...], product.astype(jnp.bfloat16), preferred_element_type=jnp.float32
             )
+            for part in range(parts):
+                cols = slice(part * lanes, (part + 1) * lanes)
+                spectra.at[part][pl.ds(k, second, stride=padded), :] = inv[:second, cols]
+                spectra.at[part][pl.ds(k + kept, second, stride=padded), :] = inv[second:, cols]
+
+    def back_outer():
+        @pl.loop(0, second, unroll=4)
+        def _(b):
+            rows = pl.ds(pl.multiple_of(b * padded, 8), padded)
+            filled = jnp.concatenate([spectra[part, rows, :] for part in range(parts)], axis=1)
+            found = jnp.dot(back[b], filled.astype(jnp.bfloat16), preferred_element_type=jnp.float32)
+            for part in range(parts):
+                total.at[part][pl.ds(b, reach, stride=second), :] = found[
+                    :, part * lanes : (part + 1) * lanes
+                ]
+
+        @pl.loop(0, length // block)
+        def _(at):
+            rows = pl.ds(pl.multiple_of(at * block, block), block)
+            for part in range(parts):
+                result[rows, part * lanes : (part + 1) * lanes] = total[part, rows, :].astype(
+                    jnp.bfloat16
+                )
+
+    return ahead_outer, inner, back_outer
+
+
+def long_conv_kernel(dims, *refs):
+    for phase in conv_phases(dims, *refs):
+        phase()
 
 
 def long_conv(signal, taps, skip):
@@ -743,17 +646,235 @@
     )(signal, taps, skip, *tables)
 
 
+def mix_and_gather_kernel(
+    dims,
+    chan_count,
+    gated,
+    query,
+    signal,
+    taps,
+    skip,
+    outer,
+    ahead,
+    behind,
+    back,
+    full,
+    wide,
+    spectra,
+    total,
+    result,
+    crossed,
+    ready,
+    room,
+    local_sem,
+    cross_sem,
+    mate_send,
+    mate_recv,
+    line_send,
+    line_recv,
+):
+    y, s, z = (lax.axis_index(name) for name in ("groups", "seq", "chan"))
+    x, core = s // 2, s % 2
+    mate = (y, s + 1 - 2 * core, z)
+    across = (y, (1 - x) * 2 + core, z)
+    _, rows, width = gated.shape
+    half_chunks = GATED_CHUNKS // 2
+    chunk_rows = rows // half_chunks
+    greet(
+        [
+            (mate, True),
+            (across, True),
+            ((y, s, jnp.minimum(z + 1, chan_count - 1)), z + 1 < chan_count),
+            ((y, s, jnp.maximum(z - 1, 0)), z > 0),
+        ]
+    )
+
+    def column(part, owner, of):
+        return ((owner * 2 + of) * 2 + part) * width
+
+    lines = []
+    for part in range(2):
+
+        def view(owner, chunk, part=part):
+            side, at = divmod(chunk, half_chunks)
+            start = column(part, owner, core if side == 0 else 1 - core)
+            return full.at[pl.ds(at * chunk_rows, chunk_rows), pl.ds(start, width)]
+
+        lines.append(
+            Line(
+                view,
+                chan_count,
+                GATED_CHUNKS,
+                line_send.at[part],
+                line_recv.at[part],
+                lambda to: (y, s, to),
+            )
+        )
+    swaps = []
+
+    def begin(part, source):
+        line = lines[part]
+        for at in range(half_chunks):
+            piece = pl.ds(at * chunk_rows, chunk_rows)
+            copy = remote(
+                source.at[1 - core, piece],
+                full.at[piece, pl.ds(column(part, z, core), width)],
+                mate_send.at[part, at],
+                mate_recv.at[part, at],
+                mate,
+            )
+            copy.start()
+            swaps.append(copy)
+        for chunk in range(half_chunks):
+            own = source.at[core, pl.ds(chunk * chunk_rows, chunk_rows)]
+            for way in range(2):
+
+                @pl.when(line.sends(way, 0))
+                def _():
+                    line.copy(way, 0, chunk, own).start()
+
+        for at in range(half_chunks):
+            block = full.at[
+                pl.ds(at * chunk_rows, chunk_rows), pl.ds(column(part, z, 1 - core), width)
+            ]
+            remote(block, block, mate_send.at[part, at], mate_recv.at[part, at], mate).wait_recv()
+            for way in range(2):
+
+                @pl.when(line.sends(way, 0))
+                def _():
+                    line.copy(way, 0, half_chunks + at).start()
+
+    def relay(part, step):
+        line = lines[part]
+        for chunk in range(GATED_CHUNKS):
+            for way in range(2):
+
+                @pl.when(line.receives(way, step))
+                def _():
+                    line.arrived(way, step, chunk)
+
+                if step + 1 < chan_count - 1:
+
+                    @pl.when(line.receives(way, step) & line.sends(way, step + 1))
+                    def _():
+                        line.copy(way, step + 1, chunk).start()
+
+    ahead_outer, inner, back_outer = conv_phases(
+        dims, signal, taps, skip, outer, ahead, behind, back, result, wide, spectra, total
+    )
+    take = pltpu.make_async_copy(gated.at[core], room, local_sem.at[0])
+    take.start()
+    begin(0, gated)
+    take.wait()
+    put = pltpu.make_async_copy(
+        room, full.at[:, pl.ds(column(0, z, core), width)], local_sem.at[1]
+    )
+    put.start()
+    ahead_outer()
+    inner()
+    relay(0, 0)
+    back_outer()
+    positions = 2 * rows
+    cross = remote(
+        result.at[pl.ds((1 - x) * positions, positions)],
+        crossed,
+        cross_sem.at[0],
+        cross_sem.at[1],
+        across,
+    )
+    cross.start()
+    for step in range(1, chan_count - 2):
+        relay(0, step)
+    cross.wait()
+    block = 64
+    share = width // 2
+
+    @pl.loop(0, positions // block)
+    def _(at):
+        start = pl.multiple_of(at * block, block)
+        mine = result[pl.ds(pl.multiple_of(x * positions + start, block), block), :]
+        other = crossed[pl.ds(start, block), :]
+        low = jnp.where(x == 0, mine.astype(jnp.float32), other.astype(jnp.float32))
+        high = jnp.where(x == 0, other.astype(jnp.float32), mine.astype(jnp.float32))
+        asked = query[pl.ds(start, block), :].astype(jnp.float32)
+        to = at // (rows // block)
+        row = pl.ds(pl.multiple_of((at - to * (rows // block)) * block, block), block)
+        ready[to, row, :share] = (asked[:, :share] * low).astype(jnp.bfloat16)
+        ready[to, row, share:] = (asked[:, share:] * high).astype(jnp.bfloat16)
+
+    begin(1, ready)
+    last = pltpu.make_async_copy(
+        ready.at[core], full.at[:, pl.ds(column(1, z, core), width)], local_sem.at[2]
+    )
+    last.start()
+    relay(0, chan_count - 2)
+    for step in range(chan_count - 1):
+        relay(1, step)
+    put.wait()
+    last.wait()
+    for copy in swaps:
+        copy.wait_send()
+    for line in lines:
+        for step in range(chan_count - 1):
+            for chunk in range(GATED_CHUNKS):
+                for way in range(2):
+
+                    @pl.when(line.sends(way, step))
+                    def _():
+                        line.copy(way, step, chunk).wait_send()
+
+
+def mix_and_gather(gated, query, signal, taps, skip, chan_count):
+    _, rows, width = gated.shape
+    length, lanes = signal.shape
+    first, second, kept, padded, tables = fourier_tables(length)
+    dma = pltpu.SemaphoreType.DMA
+    half_chunks = GATED_CHUNKS // 2
+    vmem = pl.BlockSpec(memory_space=pltpu.VMEM)
+    return pl.pallas_call(
+        functools.partial(
+            mix_and_gather_kernel, (first, second, kept, padded), chan_count
+        ),
+        out_shape=jax.ShapeDtypeStruct((rows, 4 * chan_count * width), gated.dtype),
+        in_specs=[ANY] + [vmem] * 8,
+        out_specs=ANY,
+        scratch_shapes=[
+            pltpu.VMEM((2 * lanes // 128, length, 128), jnp.float32),
+            pltpu.VMEM((2 * lanes // 128, second * padded, 128), jnp.float32),
+            pltpu.VMEM((lanes // 128, length, 128), jnp.float32),
+            pltpu.VMEM((length, lanes), jnp.bfloat16),
+            pltpu.VMEM((2 * rows, lanes), jnp.bfloat16),
+            pltpu.VMEM((2, rows, width), jnp.bfloat16),
+            pltpu.VMEM((rows, width), gated.dtype),
+            dma((3,)),
+            dma((2,)),
+            dma((2, half_chunks)),
+            dma((2, half_chunks)),
+            dma((2, 2, chan_count - 1, GATED_CHUNKS)),
+            dma((2, 2, chan_count - 1, GATED_CHUNKS)),
+        ],
+        compiler_params=pltpu.CompilerParams(
+            collective_id=1, has_side_effects=True, vmem_limit_bytes=48 * 1024 * 1024
+        ),
+        name="mix_and_gather",
+    )(gated, query, signal, taps, skip, *tables)
+
+
 def chip_body(tokens, norm_gain, proj_weight, short_filter, long_filter, skip_gain, out_weight):
     seq_count, chan_count = lax.axis_size("seq"), lax.axis_size("chan")
     rows, width = tokens.shape
     depth, branches, local_chan = proj_weight.shape
     half = local_chan // 2
     share = half // 2
+    lanes = share // 2
     s = lax.axis_index("seq")
     x, core = s // 2, s % 2
     weights = proj_weight.transpose(1, 0, 2)
     taps = (
-        long_filter.astype(jnp.bfloat16).reshape(2, 2, share, rows).transpose(0, 1, 3, 2)
+        long_filter.astype(jnp.bfloat16)
+        .reshape(2, 2, 2, lanes, rows)
+        .transpose(0, 2, 4, 1, 3)
+        .reshape(2, 2, rows, share)
     )
     whole, all_weights, all_taps = gather_inputs(tokens, weights, taps, chan_count)
     wide = whole.astype(jnp.float32)
@@ -779,27 +900,35 @@
     ).astype(jnp.bfloat16)
     swap = [(at, (at + 2) % seq_count) for at in range(seq_count)]
     near = x == 0
-    skip = lax.dynamic_slice_in_dim(skip_gain, core * half + x * share, share, 0)
-    lanes = 128
-    found = []
-    for at in range(share // lanes):
-        cols = slice(at * lanes, (at + 1) * lanes)
-        left, right = middle[:, cols], middle[:, share:][:, cols]
+    skip = lax.dynamic_slice_in_dim(skip_gain, core * half, half, 0).reshape(2, 2, lanes)
+    skip = lax.dynamic_index_in_dim(skip, x, 1, keepdims=False)
+    signals = []
+    for part in range(2):
+        pair = middle[:, part * share : (part + 1) * share]
+        left, right = pair[:, :lanes], pair[:, lanes:]
         kept = jnp.where(near, left, right)
         other = lax.ppermute(jnp.where(near, right, left), "seq", swap)
-        signal = jnp.concatenate(
-            [jnp.where(near, kept, other), jnp.where(near, other, kept)], axis=0
+        signals.append(
+            jnp.concatenate([jnp.where(near, kept, other), jnp.where(near, other, kept)], axis=0)
         )
-        longer = long_conv(signal, all_taps[:, cols], skip[None, cols])
-        early, late = longer[: 2 * rows], longer[2 * rows :]
-        kept = jnp.where(near, early, late)
-        other = lax.ppermute(jnp.where(near, late, early), "seq", swap)
-        found.append((jnp.where(near, kept, other), jnp.where(near, other, kept)))
-    longer = jnp.concatenate([part[0] for part in found] + [part[1] for part in found], axis=1)
-    gated = (featured[:, :half].astype(jnp.float32) * longer.astype(jnp.float32)).astype(
+    longer = long_conv(signals[0], all_taps[:, :lanes], skip[:1])
+    early, late = longer[: 2 * rows], longer[2 * rows :]
+    kept = jnp.where(near, early, late)
+    other = lax.ppermute(jnp.where(near, late, early), "seq", swap)
+    longer = jnp.concatenate(
+        [jnp.where(near, kept, other), jnp.where(near, other, kept)], axis=1
+    )
+    gated = (featured[:, :share].astype(jnp.float32) * longer.astype(jnp.float32)).astype(
         jnp.bfloat16
     )
-    full_mix = gather_gated(gated.reshape(2, rows, half), chan_count)
+    full_mix = mix_and_gather(
+        gated.reshape(2, rows, share),
+        featured[:, share:half],
+        signals[1],
+        all_taps[:, lanes:],
+        skip[1:],
+        chan_count,
+    )
     update = jnp.dot(full_mix, out_weight, preferred_element_type=jnp.float32)
     return (tokens.astype(jnp.float32) + update).astype(jnp.bfloat16)
 

time: 264 us -> 248 us (0.939)
  Pallas kernels: 195 us -> 180 us
  waiting for transfers between devices: 8.54 us -> 13.9 us
  other arithmetic: 18.6 us -> 14.6 us
    pallas_call x2 -> x1, Pallas kernels: 33.4 us -> 16.7 us  [long_conv(): pl.pallas_call(functools.partial(long_conv_kernel, (first, second, kept,...]
    ppermute x2, waiting for transfers between devices: 2.94 us -> 9.24 us  [chip_body(): other = lax.ppermute(jnp.where(near, right, left), 'seq', swap)]
  transfers between devices with their start and end apart: 5 -> 4, of which waited for: 3 -> 4; matrix products, arithmetic and copies ran while one was open for 2% -> 1% of each run, Pallas kernels for 13% -> 0%
where the time goes in v3:
time: 248 us
  Pallas kernels  180 us (73%)
  matrix products  26 us (10%)
  other arithmetic  14.6 us (6%)
  waiting for transfers between devices  13.9 us (6%)
  starting transfers between devices  7.67 us (3%)
  local copies, waits for them, and re-layouts  5.51 us (2%)
    pallas_call x1, Pallas kernels, gather_inputs(): pl.pallas_call(functools.partial(gather_inputs_kernel, chan_count), out_s...  89.9 us
    pallas_call x1, Pallas kernels, mix_and_gather(): pl.pallas_call(functools.partial(mix_and_gather_kernel, (first, second, k...  73 us
    pallas_call x1, Pallas kernels, long_conv(): pl.pallas_call(functools.partial(long_conv_kernel, (first, second, kept,...  16.7 us
    dot_general x1, matrix products, chip_body(): jnp.dot(normed, all_weights, preferred_element_type=jnp.float32)  15.9 us
    dot_general x1, matrix products, chip_body(): update = jnp.dot(full_mix, out_weight, preferred_element_type=jnp.float32)  10.1 us
    ppermute x2, waiting for transfers between devices, chip_body(): other = lax.ppermute(jnp.where(near, right, left), 'seq', swap)  9.24 us
    reduce_sum x1, other arithmetic, chip_body(): jnp.mean(wide * wide, axis=1, keepdims=True) + EPSILON  5.22 us
  transfers between devices with their start and end apart: 4, of which 4 were waited for; matrix products, arithmetic and copies ran while one was open for 1% of the time, Pallas kernels for 0%

profile of v3, /device:TPU:0, one launch (start us, length us, event | category | flops | bytes accessed | tf_op | source)
XLA Modules:
  0.0 247.6 jit_solution(6176383136638105357)
XLA Ops:
  0.0 1.7 convert_element_type.43
  1.7 0.8 copy.16
  2.5 1.5 reshape.31.taps
  4.0 89.9 %gather_inputs.1 = (bf16[1024,4096]{1,0:T(8,128)(2,1)}, bf16[4096,1536]{1,0:T(8,128)(2,1)}, bf16[2048,256]{1,0:T(8,128)(2,1)}) custom-call(bf16[512,1024]{1,0:T(8,128)(2,1)} %tokens.1, bf16[3,1024,1024]{2,1,0:T(8,128)(2,1)} %bitcast.13, bf16[2,2,512,256]{3,2,1,0:T(8,128)(2,1)} %reshape.31.taps), custom_call_target="tpu_custom_call" | custom-call | tf_op jit(solution)/shard_map/gather_inputs/pallas_call | solution.py:483
  94.0 5.2 %fusion = f32[1024]{0:T(1024)S(1)} fusion(bf16[1024,4096]{1,0:T(8,128)(2,1)} %get-tuple-element.8), kind=kLoop, calls=%fused_computation.2 | loop fusion | flops 12581888 | bytes 8392704 | tf_op jit(solution)/shard_map/reduce_sum | solution.py:882
  99.7 15.9 %fusion.10 = bf16[1024,1536]{1,0:T(8,128)(2,1)S(1)} fusion(bf16[4096,1536]{1,0:T(8,128)(2,1)} %get-tuple-element.9, bf16[1024,4096]{1,0:T(8,128)(2,1)S(1)} %copy-done.5, f32[4096]{0:T(1024)S(1)} %copy-done.10, f32[1024]{0:T(1024)S(1)} %add_rsqrt_fusion), kind=kOutput, calls=%fused_computation.14 | convolution fusion | flops 12903251968 | bytes 24137728 | tf_op jit(solution)/shard_map/dot_general | solution.py:884
  115.7 3.4 %collective-permute-start = (bf16[2,1536]{1,0:T(2,128)(2,1)S(1)}, bf16[2,1536]{1,0:T(2,128)(2,1)S(1)}, u32[]{:S(2)}, u32[]{:S(2)}) collective-permute-start(bf16[2,1536]{1,0:T(2,128)(2,1)S(1)} %slice.101), channel_id=1, source_target_pairs={{0,8},{4,12},{1,9},{5,13},{2,10},{6,14},{3,11},{7,15},{16,24},{20,... | collective-permute-start | bytes 18440 | tf_op jit(solution)/shard_map/ppermute | solution.py:22
  119.2 1.0 collective-permute-done
  120.3 0.9 maximum_convert_fusion
  121.2 2.0 fusion.8
  123.6 2.3 collective-permute-start.3
  126.1 0.9 fusion.15
  127.6 5.6 %collective-permute-done.3 = bf16[1024,128]{1,0:T(8,128)(2,1)S(1)} collective-permute-done((bf16[1024,128]{1,0:T(8,128)(2,1)S(1)}, bf16[1024,128]{1,0:T(8,128)(2,1)S(1)}, u32[]{:S(2)}, u32[]{:S(2)}) %collective-permute-start.3) | collective-permute-done | bytes 262176 | tf_op jit(solution)/shard_map/ppermute | solution.py:910
  133.1 3.7 %collective-permute-done.1 = bf16[1024,128]{1,0:T(8,128)(2,1)S(1)} collective-permute-done((bf16[1024,128]{1,0:T(8,128)(2,1)S(1)}, bf16[1024,128]{1,0:T(8,128)(2,1)S(1)}, u32[]{:S(2)}, u32[]{:S(2)}) %collective-permute-start.1) | collective-permute-done | bytes 262176 | tf_op jit(solution)/shard_map/ppermute | solution.py:910
  137.0 0.9 pad_maximum_fusion
  137.8 16.7 %long_conv.1 = bf16[2048,128]{1,0:T(8,128)(2,1)} custom-call(bf16[2048,128]{1,0:T(8,128)(2,1)} %get-tuple-element.28.refs_0_, bf16[2048,128]{1,0:T(8,128)(2,1)} %get-tuple-element.16.refs_1_, f32[1,128]{1,0:T(1,128)} %get-tuple-element.27.refs_2_, bf16[64,72,32]{2,1,0:T(8,128)(2,1)} %constant.53.clone.refs_3_.outer, ...), custom_call_target="tpu_custom_call" | custom-call | flops 1342177280 | bytes 1572864 | tf_op jit(solution)/shard_map/long_conv/pallas_call | solution.py:633
  154.5 1.1 broadcast_select_fusion.6
  155.7 1.8 collective-permute-start.2
  157.5 1.1 slice.112.query
  158.5 3.6 %collective-permute-done.2 = bf16[1024,128]{1,0:T(8,128)(2,1)S(1)} collective-permute-done((bf16[1024,128]{1,0:T(8,128)(2,1)S(1)}, bf16[1024,128]{1,0:T(8,128)(2,1)S(1)}, u32[]{:S(2)}, u32[]{:S(2)}) %collective-permute-start.2) | collective-permute-done | bytes 262176 | tf_op jit(solution)/shard_map/ppermute | solution.py:917
  162.1 1.1 broadcast_select_fusion.5
  163.2 1.2 multiply_convert_fusion.1
  164.4 73.0 %mix_and_gather.1 = bf16[512,4096]{1,0:T(8,128)(2,1)} custom-call(bf16[2,512,256]{2,1,0:T(8,128)(2,1)S(1)} %bitcast.12, bf16[1024,256]{1,0:T(8,128)(2,1)S(1)} %slice.112.query, bf16[2048,128]{1,0:T(8,128)(2,1)S(1)} %get-tuple-element.29.signal, bf16[2048,128]{1,0:T(8,128)(2,1)S(1)} %get-tuple-element.15.taps, f32[1,128]{1,0:T(1,128)S(1)} %get-tuple-element.26.skip, ...), custom_call_target="tpu_custom_call" | custom-call | tf_op jit(solution)/shard_map/mix_and_gather/pallas_call | solution.py:834
  237.5 10.1 %add_convert_fusion = bf16[512,1024]{1,0:T(8,128)(2,1)} fusion(bf16[512,1024]{1,0:T(8,128)(2,1)S(1)} %copy-done.7, bf16[512,4096]{1,0:T(8,128)(2,1)} %mix_and_gather.1, bf16[4096,1024]{1,0:T(8,128)(2,1)} %param.21), kind=kOutput, calls=%fused_computation.16 | convolution fusion | flops 4296540160 | bytes 14680064 | tf_op jit(solution)/shard_map/dot_general | solution.py:932
  (34 shorter events, 1.8 us)
Async XLA Ops:
  4.0 95.2 %copy-start.10 = (f32[4096]{0:T(1024)S(1)}, f32[4096]{0:T(1024)}, u32[]{:S(2)}) copy-start(f32[4096]{0:T(1024)} %param.16) | copy-start | bytes 49156
  94.0 5.8 %copy-start.5 = (bf16[1024,4096]{1,0:T(8,128)(2,1)S(1)}, bf16[1024,4096]{1,0:T(8,128)(2,1)}, u32[]{:S(2)}) copy-start(bf16[1024,4096]{1,0:T(8,128)(2,1)} %get-tuple-element.8) | copy-start | bytes 25165828
  99.7 19.4 %copy-start.8 = (f32[3,3,1024]{2,1,0:T(4,128)S(1)}, f32[3,3,1024]{2,1,0:T(4,128)}, u32[]{:S(2)}) copy-start(f32[3,3,1024]{2,1,0:T(4,128)} %param.18) | copy-start | bytes 110596
  115.7 4.6 %collective-permute-start = (bf16[2,1536]{1,0:T(2,128)(2,1)S(1)}, bf16[2,1536]{1,0:T(2,128)(2,1)S(1)}, u32[]{:S(2)}, u32[]{:S(2)}) collective-permute-start(bf16[2,1536]{1,0:T(2,128)(2,1)S(1)} %slice.101), channel_id=1, source_target_pairs={{0,8},{4,12},{1,9},{5,13},{2,10},{6,14},{3,11},{7,15},{16,24},{20,... | collective-permute-start | bytes 18440 | tf_op jit(solution)/shard_map/ppermute | solution.py:22
  121.2 4.8 %copy-start.6 = (bf16[2048,256]{1,0:T(8,128)(2,1)S(1)}, bf16[2048,256]{1,0:T(8,128)(2,1)}, u32[]{:S(2)}) copy-start(bf16[2048,256]{1,0:T(8,128)(2,1)} %get-tuple-element.10) | copy-start | bytes 3145732
  123.2 2.8 %copy-start.4 = (bf16[1024,1536]{1,0:T(8,128)(2,1)}, bf16[1024,1536]{1,0:T(8,128)(2,1)S(1)}, u32[]{:S(2)}) copy-start(bf16[1024,1536]{1,0:T(8,128)(2,1)S(1)} %fusion.8) | copy-start | bytes 9437188
  123.2 3.7 %copy-start.9 = (f32[1024]{0:T(1024)S(1)}, f32[1024]{0:T(1024)}, u32[]{:S(2)}) copy-start(f32[1024]{0:T(1024)} %param.20) | copy-start | bytes 12292
  123.6 9.5 %collective-permute-start.3 = (bf16[1024,128]{1,0:T(8,128)(2,1)S(1)}, bf16[1024,128]{1,0:T(8,128)(2,1)S(1)}, u32[]{:S(2)}, u32[]{:S(2)}) collective-permute-start(bf16[1024,128]{1,0:T(8,128)(2,1)S(1)} %get-tuple-element.19), channel_id=1, source_target_pairs={{0,8},{4,12},{8,0},{12,4},{1,9},{5,13},{9,1},{13,5},{2,10},{6,14},... | collective-permute-start | bytes 786440 | tf_op jit(solution)/shard_map/ppermute | solution.py:910
  126.0 10.9 %collective-permute-start.1 = (bf16[1024,128]{1,0:T(8,128)(2,1)S(1)}, bf16[1024,128]{1,0:T(8,128)(2,1)S(1)}, u32[]{:S(2)}, u32[]{:S(2)}) collective-permute-start(bf16[1024,128]{1,0:T(8,128)(2,1)S(1)} %get-tuple-element.20), channel_id=1, source_target_pairs={{0,8},{4,12},{8,0},{12,4},{1,9},{5,13},{9,1},{13,5},{2,10},{6,14},... | collective-permute-start | bytes 786440 | tf_op jit(solution)/shard_map/ppermute | solution.py:910
  136.9 27.5 %copy-start = (bf16[64,72,32]{2,1,0:T(8,128)(2,1)S(1)}, bf16[64,72,32]{2,1,0:T(8,128)(2,1)}, u32[]{:S(2)}) copy-start(bf16[64,72,32]{2,1,0:T(8,128)(2,1)} %constant.53.clone.refs_3_.outer) | copy-start | bytes 884740
  136.9 27.5 %copy-start.1 = (bf16[64,32,72]{2,1,0:T(8,128)(2,1)S(1)}, bf16[64,32,72]{2,1,0:T(8,128)(2,1)}, u32[]{:S(2)}) copy-start(bf16[64,32,72]{2,1,0:T(8,128)(2,1)} %constant.56.clone.refs_6_.back) | copy-start | bytes 884740
  136.9 27.5 %copy-start.2 = (bf16[128,128]{1,0:T(8,128)(2,1)S(1)}, bf16[128,128]{1,0:T(8,128)(2,1)}, u32[]{:S(2)}) copy-start(bf16[128,128]{1,0:T(8,128)(2,1)} %constant.54.clone.refs_4_.ahead) | copy-start | bytes 98308
  137.0 27.5 %copy-start.3 = (bf16[128,128]{1,0:T(8,128)(2,1)S(1)}, bf16[128,128]{1,0:T(8,128)(2,1)}, u32[]{:S(2)}) copy-start(bf16[128,128]{1,0:T(8,128)(2,1)} %constant.55.clone.refs_5_.behind) | copy-start | bytes 98308
  154.5 83.0 %copy-start.7 = (bf16[512,1024]{1,0:T(8,128)(2,1)S(1)}, bf16[512,1024]{1,0:T(8,128)(2,1)}, u32[]{:S(2)}) copy-start(bf16[512,1024]{1,0:T(8,128)(2,1)} %tokens.1) | copy-start | bytes 3145732
  155.7 6.5 %collective-permute-start.2 = (bf16[1024,128]{1,0:T(8,128)(2,1)S(1)}, bf16[1024,128]{1,0:T(8,128)(2,1)S(1)}, u32[]{:S(2)}, u32[]{:S(2)}) collective-permute-start(bf16[1024,128]{1,0:T(8,128)(2,1)S(1)} %broadcast_select_fusion.6), channel_id=1, source_target_pairs={{0,8},{4,12},{8,0},{12,4},{1,9},{5,13},{9,1},{13,5},{2,10},{6,14},... | collective-permute-start | bytes 786440 | tf_op jit(solution)/shard_map/ppermute | solution.py:917

commit v4 on v3

--- a/solution.py
+++ b/solution.py
@@ -297,6 +297,16 @@
             def _():
                 line.copy(way, 0, chunk, own).start()
 
+    for to in range(2):
+        copy = remote(
+            taps.at[to, 1 - x, pl.ds(y * half_lags, half_lags)],
+            tap_view(s, y),
+            f_send.at[to],
+            f_recv.at[core],
+            across(to),
+        )
+        copy.start()
+        pending.append(copy)
     for chunk in range(WEIGHT_CHUNKS):
         for to in range(2):
             view = weight_view(s, y, chunk)
@@ -315,16 +325,6 @@
             pending.append(
                 remote(view, view, x_send.at[to, chunk], x_recv.at[core, chunk], across(to))
             )
-    for to in range(2):
-        copy = remote(
-            taps.at[to, 1 - x, pl.ds(y * half_lags, half_lags)],
-            tap_view(s, y),
-            f_send.at[to],
-            f_recv.at[core],
-            across(to),
-        )
-        copy.start()
-        pending.append(copy)
     own_view = all_tokens.at[pl.ds(core * rows, rows), pl.ds(z * width, width)]
     mate_copies = [
         remote(tokens, own_view, mate_send.at[0], mate_recv.at[0], mate),
@@ -386,6 +386,13 @@
         index = 3 + (way * (chan_count - 1) + step) * TOKEN_CHUNKS + chunk
         return remote(block, block, mate_send.at[index], mate_recv.at[index], mate)
 
+    for origin in range(2):
+        view = tap_view((1 - x) * 2 + origin, y)
+        remote(view, view, f_send.at[origin], f_recv.at[origin], beside).wait_recv()
+        copy = remote(view, view, f_send.at[2 + origin], f_recv.at[2 + origin], beside)
+        copy.start()
+        pending.append(copy)
+
     steps = (chan_count - 1) * TOKEN_CHUNKS
     forwarded = 0
     for at in range(steps):
@@ -417,13 +424,6 @@
                 copy.start()
                 pending.append(copy)
             forwarded += 1
-    for origin in range(2):
-        view = tap_view((1 - x) * 2 + origin, y)
-        remote(view, view, f_send.at[origin], f_recv.at[origin], beside).wait_recv()
-        copy = remote(view, view, f_send.at[2 + origin], f_recv.at[2 + origin], beside)
-        copy.start()
-        pending.append(copy)
-
     for origin in range(2):
         owner = (1 - x) * 2 + origin
         for chunk in range(WEIGHT_CHUNKS):
@@ -902,16 +902,21 @@
     near = x == 0
     skip = lax.dynamic_slice_in_dim(skip_gain, core * half, half, 0).reshape(2, 2, lanes)
     skip = lax.dynamic_index_in_dim(skip, x, 1, keepdims=False)
-    signals = []
-    for part in range(2):
-        pair = middle[:, part * share : (part + 1) * share]
+    def joined(pair, other):
         left, right = pair[:, :lanes], pair[:, lanes:]
         kept = jnp.where(near, left, right)
-        other = lax.ppermute(jnp.where(near, right, left), "seq", swap)
-        signals.append(
-            jnp.concatenate([jnp.where(near, kept, other), jnp.where(near, other, kept)], axis=0)
+        return jnp.concatenate(
+            [jnp.where(near, kept, other), jnp.where(near, other, kept)], axis=0
         )
-    longer = long_conv(signals[0], all_taps[:, :lanes], skip[:1])
+
+    pairs = [middle[:, :share], middle[:, share:]]
+    others = [
+        lax.ppermute(jnp.where(near, pair[:, lanes:], pair[:, :lanes]), "seq", swap)
+        for pair in pairs
+    ]
+    longer = long_conv(joined(pairs[0], others[0]), all_taps[:, :lanes], skip[:1])
+    longer, later = lax.optimization_barrier((longer, others[1]))
+    signal = joined(pairs[1], later)
     early, late = longer[: 2 * rows], longer[2 * rows :]
     kept = jnp.where(near, early, late)
     other = lax.ppermute(jnp.where(near, late, early), "seq", swap)
@@ -924,7 +929,7 @@
     full_mix = mix_and_gather(
         gated.reshape(2, rows, share),
         featured[:, share:half],
-        signals[1],
+        signal,
         all_taps[:, lanes:],
         skip[1:],
         chan_count,

time: 248 us -> 242 us (0.976)
  waiting for transfers between devices: 13.9 us -> 10.4 us
    ppermute x2, waiting for transfers between devices: 9.24 us -> 3.28 us  [chip_body(): lax.ppermute(jnp.where(near, pair[:, lanes:], pair[:, :lanes]), 'seq', swap)]
  transfers between devices with their start and end apart: 4 -> 4, of which waited for: 4 -> 3; matrix products, arithmetic and copies ran while one was open for 1% -> 1% of each run, Pallas kernels for 0% -> 7%
where the time goes in v4:
time: 242 us
  Pallas kernels  178 us (74%)
  matrix products  26 us (11%)
  other arithmetic  14.6 us (6%)
  waiting for transfers between devices  10.4 us (4%)
  starting transfers between devices  7.2 us (3%)
  local copies, waits for them, and re-layouts  5.48 us (2%)
    pallas_call x1, Pallas kernels, gather_inputs(): pl.pallas_call(functools.partial(gather_inputs_kernel, chan_count), out_s...  88.2 us
    pallas_call x1, Pallas kernels, mix_and_gather(): pl.pallas_call(functools.partial(mix_and_gather_kernel, (first, second, k...  72.9 us
    pallas_call x1, Pallas kernels, long_conv(): pl.pallas_call(functools.partial(long_conv_kernel, (first, second, kept,...  16.7 us
    dot_general x1, matrix products, chip_body(): jnp.dot(normed, all_weights, preferred_element_type=jnp.float32)  15.9 us
    dot_general x1, matrix products, chip_body(): update = jnp.dot(full_mix, out_weight, preferred_element_type=jnp.float32)  10.1 us
    ppermute x1, waiting for transfers between devices, chip_body(): other = lax.ppermute(jnp.where(near, late, early), 'seq', swap)  6.05 us
    reduce_sum x1, other arithmetic, chip_body(): jnp.mean(wide * wide, axis=1, keepdims=True) + EPSILON  5.22 us
  transfers between devices with their start and end apart: 4, of which 3 were waited for; matrix products, arithmetic and copies ran while one was open for 1% of the time, Pallas kernels for 7%

profile of v4, /device:TPU:0, one launch (start us, length us, event | category | flops | bytes accessed | tf_op | source)
XLA Modules:
  0.0 241.7 jit_solution(18159319055310198759)
XLA Ops:
  0.0 1.7 convert_element_type.43
  1.7 0.8 copy.16
  2.5 1.5 reshape.31.taps
  4.0 88.2 %gather_inputs.1 = (bf16[1024,4096]{1,0:T(8,128)(2,1)}, bf16[4096,1536]{1,0:T(8,128)(2,1)}, bf16[2048,256]{1,0:T(8,128)(2,1)}) custom-call(bf16[512,1024]{1,0:T(8,128)(2,1)} %tokens.1, bf16[3,1024,1024]{2,1,0:T(8,128)(2,1)} %bitcast.13, bf16[2,2,512,256]{3,2,1,0:T(8,128)(2,1)} %reshape.31.taps), custom_call_target="tpu_custom_call" | custom-call | tf_op jit(solution)/shard_map/gather_inputs/pallas_call | solution.py:483
  92.2 5.2 %fusion = f32[1024]{0:T(1024)S(1)} fusion(bf16[1024,4096]{1,0:T(8,128)(2,1)} %get-tuple-element.10), kind=kLoop, calls=%fused_computation.2 | loop fusion | flops 12581888 | bytes 8392704 | tf_op jit(solution)/shard_map/reduce_sum | solution.py:882
  98.0 15.9 %fusion.10 = bf16[1024,1536]{1,0:T(8,128)(2,1)S(1)} fusion(bf16[4096,1536]{1,0:T(8,128)(2,1)} %get-tuple-element.11, bf16[1024,4096]{1,0:T(8,128)(2,1)S(1)} %copy-done.5, f32[4096]{0:T(1024)S(1)} %copy-done.10, f32[1024]{0:T(1024)S(1)} %add_rsqrt_fusion), kind=kOutput, calls=%fused_computation.14 | convolution fusion | flops 12903251968 | bytes 24137728 | tf_op jit(solution)/shard_map/dot_general | solution.py:884
  113.9 2.7 %collective-permute-start = (bf16[2,1536]{1,0:T(2,128)(2,1)S(1)}, bf16[2,1536]{1,0:T(2,128)(2,1)S(1)}, u32[]{:S(2)}, u32[]{:S(2)}) collective-permute-start(bf16[2,1536]{1,0:T(2,128)(2,1)S(1)} %slice.105), channel_id=1, source_target_pairs={{0,8},{4,12},{1,9},{5,13},{2,10},{6,14},{3,11},{7,15},{16,24},{20,... | collective-permute-start | bytes 18440 | tf_op jit(solution)/shard_map/ppermute | solution.py:22
  116.7 1.0 collective-permute-done
  117.8 0.9 maximum_convert_fusion
  118.7 2.0 fusion.8
  121.1 2.3 collective-permute-start.1
  123.5 0.9 fusion.15
  124.4 0.5 fusion.13
  124.9 1.1 slice.116.query
  126.0 3.3 %collective-permute-done.1 = bf16[1024,128]{1,0:T(8,128)(2,1)S(1)} collective-permute-done((bf16[1024,128]{1,0:T(8,128)(2,1)S(1)}, bf16[1024,128]{1,0:T(8,128)(2,1)S(1)}, u32[]{:S(2)}, u32[]{:S(2)}) %collective-permute-start.1) | collective-permute-done | bytes 262176 | tf_op jit(solution)/shard_map/ppermute | solution.py:914
  129.4 1.8 collective-permute-start.2
  131.2 0.8 pad_maximum_fusion.refs_0_
  132.1 16.7 %long_conv.1 = bf16[2048,128]{1,0:T(8,128)(2,1)} custom-call(bf16[2048,128]{1,0:T(8,128)(2,1)} %pad_maximum_fusion.refs_0_, bf16[2048,128]{1,0:T(8,128)(2,1)} %get-tuple-element.20.refs_1_, f32[1,128]{1,0:T(1,128)} %get-tuple-element.28.refs_2_, bf16[64,72,32]{2,1,0:T(8,128)(2,1)} %constant.53.clone.refs_3_.outer, ...), custom_call_target="tpu_custom_call" | custom-call | flops 1342177280 | bytes 1572864 | tf_op jit(solution)/shard_map/long_conv/pallas_call | solution.py:633
  148.8 1.1 broadcast_select_fusion.5
  150.3 6.1 %collective-permute-done.3 = bf16[1024,128]{1,0:T(8,128)(2,1)S(1)} collective-permute-done((bf16[1024,128]{1,0:T(8,128)(2,1)S(1)}, bf16[1024,128]{1,0:T(8,128)(2,1)S(1)}, u32[]{:S(2)}, u32[]{:S(2)}) %collective-permute-start.3) | collective-permute-done | bytes 262176 | tf_op jit(solution)/shard_map/ppermute | solution.py:922
  156.3 1.1 broadcast_select_fusion.4
  157.4 1.2 multiply_convert_fusion.1
  158.6 72.9 %mix_and_gather.1 = bf16[512,4096]{1,0:T(8,128)(2,1)} custom-call(bf16[2,512,256]{2,1,0:T(8,128)(2,1)S(1)} %bitcast.12, bf16[1024,256]{1,0:T(8,128)(2,1)S(1)} %slice.116.query, bf16[2048,128]{1,0:T(8,128)(2,1)S(1)} %pad_maximum_fusion.1.signal, bf16[2048,128]{1,0:T(8,128)(2,1)S(1)} %get-tuple-element.19.taps, f32[1,128]{1,0:T(1,128)S(1)} %get-tuple-element.27.skip, ...), custom_call_target="tpu_custom_call" | custom-call | tf_op jit(solution)/shard_map/mix_and_gather/pallas_call | solution.py:834
  231.6 10.1 %add_convert_fusion = bf16[512,1024]{1,0:T(8,128)(2,1)} fusion(bf16[512,1024]{1,0:T(8,128)(2,1)S(1)} %copy-done.7, bf16[512,4096]{1,0:T(8,128)(2,1)} %mix_and_gather.1, bf16[4096,1024]{1,0:T(8,128)(2,1)} %param.21), kind=kOutput, calls=%fused_computation.16 | convolution fusion | flops 4296540160 | bytes 14680064 | tf_op jit(solution)/shard_map/dot_general | solution.py:937
  (36 shorter events, 1.5 us)
Async XLA Ops:
  4.0 93.4 %copy-start.10 = (f32[4096]{0:T(1024)S(1)}, f32[4096]{0:T(1024)}, u32[]{:S(2)}) copy-start(f32[4096]{0:T(1024)} %param.16) | copy-start | bytes 49156
  92.2 5.8 %copy-start.5 = (bf16[1024,4096]{1,0:T(8,128)(2,1)S(1)}, bf16[1024,4096]{1,0:T(8,128)(2,1)}, u32[]{:S(2)}) copy-start(bf16[1024,4096]{1,0:T(8,128)(2,1)} %get-tuple-element.10) | copy-start | bytes 25165828
  98.0 18.7 %copy-start.8 = (f32[3,3,1024]{2,1,0:T(4,128)S(1)}, f32[3,3,1024]{2,1,0:T(4,128)}, u32[]{:S(2)}) copy-start(f32[3,3,1024]{2,1,0:T(4,128)} %param.18) | copy-start | bytes 110596
  113.9 3.9 %collective-permute-start = (bf16[2,1536]{1,0:T(2,128)(2,1)S(1)}, bf16[2,1536]{1,0:T(2,128)(2,1)S(1)}, u32[]{:S(2)}, u32[]{:S(2)}) collective-permute-start(bf16[2,1536]{1,0:T(2,128)(2,1)S(1)} %slice.105), channel_id=1, source_target_pairs={{0,8},{4,12},{1,9},{5,13},{2,10},{6,14},{3,11},{7,15},{16,24},{20,... | collective-permute-start | bytes 18440 | tf_op jit(solution)/shard_map/ppermute | solution.py:22
  118.7 4.7 %copy-start.6 = (bf16[2048,256]{1,0:T(8,128)(2,1)S(1)}, bf16[2048,256]{1,0:T(8,128)(2,1)}, u32[]{:S(2)}) copy-start(bf16[2048,256]{1,0:T(8,128)(2,1)} %get-tuple-element.12) | copy-start | bytes 3145732
  118.7 5.6 %copy-start.9 = (f32[1024]{0:T(1024)S(1)}, f32[1024]{0:T(1024)}, u32[]{:S(2)}) copy-start(f32[1024]{0:T(1024)} %param.20) | copy-start | bytes 12292
  120.8 2.7 %copy-start.4 = (bf16[1024,1536]{1,0:T(8,128)(2,1)}, bf16[1024,1536]{1,0:T(8,128)(2,1)S(1)}, u32[]{:S(2)}) copy-start(bf16[1024,1536]{1,0:T(8,128)(2,1)S(1)} %fusion.8) | copy-start | bytes 9437188
  121.1 8.2 %collective-permute-start.1 = (bf16[1024,128]{1,0:T(8,128)(2,1)S(1)}, bf16[1024,128]{1,0:T(8,128)(2,1)S(1)}, u32[]{:S(2)}, u32[]{:S(2)}) collective-permute-start(bf16[1024,128]{1,0:T(8,128)(2,1)S(1)} %broadcast_select_fusion.10), channel_id=1, source_target_pairs={{0,8},{4,12},{8,0},{12,4},{1,9},{5,13},{9,1},{13,5},{2,10},{6,14},... | collective-permute-start | bytes 786440 | tf_op jit(solution)/shard_map/ppermute | solution.py:914
  129.4 29.2 %copy-start = (bf16[64,72,32]{2,1,0:T(8,128)(2,1)S(1)}, bf16[64,72,32]{2,1,0:T(8,128)(2,1)}, u32[]{:S(2)}) copy-start(bf16[64,72,32]{2,1,0:T(8,128)(2,1)} %constant.53.clone.refs_3_.outer) | copy-start | bytes 884740
  129.4 29.2 %copy-start.1 = (bf16[64,32,72]{2,1,0:T(8,128)(2,1)S(1)}, bf16[64,32,72]{2,1,0:T(8,128)(2,1)}, u32[]{:S(2)}) copy-start(bf16[64,32,72]{2,1,0:T(8,128)(2,1)} %constant.56.clone.refs_6_.back) | copy-start | bytes 884740
  129.4 29.2 %copy-start.2 = (bf16[128,128]{1,0:T(8,128)(2,1)S(1)}, bf16[128,128]{1,0:T(8,128)(2,1)}, u32[]{:S(2)}) copy-start(bf16[128,128]{1,0:T(8,128)(2,1)} %constant.54.clone.refs_4_.ahead) | copy-start | bytes 98308
  129.4 29.2 %copy-start.3 = (bf16[128,128]{1,0:T(8,128)(2,1)S(1)}, bf16[128,128]{1,0:T(8,128)(2,1)}, u32[]{:S(2)}) copy-start(bf16[128,128]{1,0:T(8,128)(2,1)} %constant.55.clone.refs_5_.behind) | copy-start | bytes 98308
  129.4 19.3 %collective-permute-start.2 = (bf16[1024,128]{1,0:T(8,128)(2,1)S(1)}, bf16[1024,128]{1,0:T(8,128)(2,1)S(1)}, u32[]{:S(2)}, u32[]{:S(2)}) collective-permute-start(bf16[1024,128]{1,0:T(8,128)(2,1)S(1)} %get-tuple-element.21), channel_id=1, source_target_pairs={{0,8},{4,12},{8,0},{12,4},{1,9},{5,13},{9,1},{13,5},{2,10},{6,14},... | collective-permute-start | bytes 786440 | tf_op jit(solution)/shard_map/ppermute | solution.py:914
  149.8 6.5 %collective-permute-start.3 = (bf16[1024,128]{1,0:T(8,128)(2,1)S(1)}, bf16[1024,128]{1,0:T(8,128)(2,1)S(1)}, u32[]{:S(2)}, u32[]{:S(2)}) collective-permute-start(bf16[1024,128]{1,0:T(8,128)(2,1)S(1)} %broadcast_select_fusion.5), channel_id=1, source_target_pairs={{0,8},{4,12},{8,0},{12,4},{1,9},{5,13},{9,1},{13,5},{2,10},{6,14},... | collective-permute-start | bytes 786440 | tf_op jit(solution)/shard_map/ppermute | solution.py:922
  150.2 81.3 %copy-start.7 = (bf16[512,1024]{1,0:T(8,128)(2,1)S(1)}, bf16[512,1024]{1,0:T(8,128)(2,1)}, u32[]{:S(2)}) copy-start(bf16[512,1024]{1,0:T(8,128)(2,1)} %tokens.1) | copy-start | bytes 3145732
